TPU v7x, 32 devices: a whole 2x2x4 slice. The times are simulated.
32 devices in a mesh: blk: 8 (over z, y), tp: 4 (over x, core).
Axes of the slice: x: 2, y: 2, z: 4, core: 2. Of those that a mesh axis runs over, the one named last changes fastest.
Arguments:
- kv_keys: bfloat16 [32, 2048, 512], P('blk', None, 'tp'), may hold values from -6 to 6
- kv_values: bfloat16 [32, 2048, 512], P('blk', None, 'tp'), may hold values from -6 to 6
- queries: bfloat16 [32, 128, 3584], P('blk', None, 'tp'), may hold values from -170 to 170, as said below
- hidden: bfloat16 [32, 128, 3584], P('blk', None, 'tp'), may hold values from -2 to 2
- out_weight: bfloat16 [3584, 3584], P('tp'), may hold values from -0.09375 to 0.09375
- block_live: int32 [32], P('blk'), may hold values from 1 to 128
- node_tiles: int32 [32, 128], P('blk'), may hold values from 1 to 16
- left_count: int32 [8], P('blk'), may hold values from 1 to 2, as said below
- right_count: int32 [8], P('blk'), may hold values from 1 to 2, as said below
Outputs:
- balanced: bfloat16 [64, 128, 3584], P('blk', None, 'tp')
Inputs may be any that keep to these rules, and one draw needn't show every extreme that they name: `queries`: queries of the nodes. `left_count`: at most 2; some index reaches 2 in every draw. `right_count`: at most 2; some index reaches 2 in every draw.
All inputs are finite; a program needn't handle non-finite values.
Results may differ from a plain program's by a relative error of at most 0.0047.
Values may be sent and summed in bfloat16 or wider, within the bound.
No kernel may reach another device: no remote copies, remote signals or barrier semaphores. Data moves between devices by JAX's collectives and lax.ppermute only.
A program may use at most 192 MiB of HBM per device.

v0:
```python
import jax
import jax.numpy as jnp
from jax import lax
from jax.sharding import PartitionSpec as P

TILE = 128
S_MAX = 2


def passed_along(value, axis, steps):
    count = lax.axis_size(axis)
    pairs = [(source, (source + steps) % count) for source in range(count)]
    return lax.ppermute(value, axis, pairs)


def attend(query_rows, key_rows, value_rows, tiles):
    batch_size, node_count, row_width = query_rows.shape
    head_size = key_rows.shape[2]
    group_size = row_width // head_size
    flat_rows = query_rows.reshape(batch_size, node_count * group_size, head_size)
    scores = jnp.einsum(
        "srd,spd->srp", flat_rows, key_rows, preferred_element_type=jnp.float32
    ) * head_size ** (-0.5)
    reach = jnp.repeat(tiles, group_size, axis=1) * TILE
    places = lax.broadcasted_iota(jnp.int32, (1, 1, key_rows.shape[1]), 2)
    inside = places < reach[:, :, None]
    scores = jnp.where(inside, scores, jnp.float32(-1e30))
    row_max = jnp.max(scores, axis=-1, keepdims=True)
    weights_exp = jnp.where(inside, jnp.exp(scores - row_max), jnp.float32(0.0))
    weights = (weights_exp / jnp.sum(weights_exp, axis=-1, keepdims=True)).astype(jnp.bfloat16)
    mixed = jnp.einsum("srp,spd->srd", weights, value_rows, preferred_element_type=jnp.float32)
    return mixed.astype(jnp.bfloat16).reshape(batch_size, node_count, row_width)


def finish(attn, residual, live_counts, out_weight):
    batch_size, node_count, row_width = attn.shape
    flat_attn = attn.reshape(batch_size * node_count, row_width)
    partial_value = jnp.dot(flat_attn, out_weight, preferred_element_type=jnp.float32)
    summed = lax.psum_scatter(partial_value, "tp", scatter_dimension=1, tiled=True)
    node_out = residual.astype(jnp.float32) + summed.reshape(residual.shape)
    node_live = jnp.arange(node_count, dtype=jnp.int32)[None, :] < live_counts[:, None]
    return jnp.where(node_live[:, :, None], node_out, jnp.float32(0.0))


def slot_usable(prev_right, own_left, own_right, next_left, block_count):
    slot_index = jnp.arange(block_count + 2 * S_MAX, dtype=jnp.int32)
    from_prev = slot_index < S_MAX
    from_next = slot_index >= S_MAX + block_count
    own_blk = slot_index - S_MAX
    own_usable = (own_blk >= own_left) & (own_blk < block_count - own_right)
    return jnp.where(
        from_prev,
        S_MAX - slot_index <= prev_right,
        jnp.where(from_next, slot_index - S_MAX - block_count < next_left, own_usable),
    )


def on_device(
    kv_keys, kv_values, queries, hidden, out_weight, block_live, node_tiles, left_count, right_count
):
    block_count = kv_keys.shape[0]
    attn = attend(queries, kv_keys, kv_values, node_tiles)
    node_out = finish(attn, hidden, block_live, out_weight).astype(jnp.bfloat16)
    from_prev = passed_along((node_out[block_count - S_MAX :], right_count), "blk", 1)
    from_next = passed_along((node_out[:S_MAX], left_count), "blk", -1)
    all_out = jnp.concatenate([from_prev[0], node_out, from_next[0]], axis=0)
    usable = slot_usable(
        from_prev[1][0], left_count[0], right_count[0], from_next[1][0], block_count
    )
    return jnp.where(usable[:, None, None], all_out, jnp.zeros((), jnp.bfloat16))


def solution(mesh):
    return jax.shard_map(
        on_device,
        mesh=mesh,
        in_specs=(
            P("blk", None, "tp"),
            P("blk", None, "tp"),
            P("blk", None, "tp"),
            P("blk", None, "tp"),
            P("tp", None),
            P("blk"),
            P("blk", None),
            P("blk"),
            P("blk"),
        ),
        out_specs=P("blk", None, "tp"),
        check_vma=False,
    )
```

profile of v0, /device:TPU:0, one launch (start us, length us, event | category | flops | bytes accessed | tf_op | source)
XLA Modules:
  0.0 219.0 jit_solution(2209409240610759397)
XLA Ops:
  6.5 0.0 copy-start
  6.5 0.0 reduce-scatter.2.cloned.1.call-start
  6.5 2.1 reshape.58
  8.7 0.7 broadcast_multiply_fusion
  9.4 0.1 broadcast_in_dim.43
  9.5 0.2 mul.22
  9.7 0.0 copy-done
  9.7 11.7 %fusion.17 = f32[4,896,2048]{2,1,0:T(8,128)} fusion(bf16[4,896,128]{2,1,0:T(8,128)(2,1)S(1)} %reshape.58, bf16[4,2048,128]{2,1,0:T(8,128)(2,1)S(1)} %copy-done), kind=kOutput, calls=%fused_computation.24 | convolution fusion | flops 1879048192 | bytes 32374784 | tf_op jit(solution)/shard_map/srd,spd->srp/dot_general | solution.py:21
  21.4 42.8 %fusion.16 = f32[4,896]{1,0:T(4,128)S(1)} fusion(f32[4,896,2048]{2,1,0:T(8,128)} %fusion.17, s32[4,896]{1,0:T(4,128)S(1)} %mul.22), kind=kOutput, calls=%fused_computation.23 | output fusion | flops 51382272 | bytes 29388800 | tf_op jit(solution)/shard_map/sub | solution.py:29
  64.2 0.0 copy-start.1
  64.2 40.3 %fusion.6 = bf16[4,896,128]{2,1,0:T(8,128)(2,1)S(1)} fusion(bf16[4,2048,128]{2,1,0:T(8,128)(2,1)} %param.10, f32[4,896]{1,0:T(4,128)S(1)} %fusion.16, f32[4,896,2048]{2,1,0:T(8,128)} %fusion.17, s32[4,896]{1,0:T(4,128)S(1)} %mul.22), kind=kOutput, calls=%fused_computation.12 | convolution fusion | flops 1938232832 | bytes 32403456 | tf_op jit(solution)/shard_map/srp,spd->srd/dot_general | solution.py:31
  104.6 1.8 reshape_reshape.3
  106.4 10.1 %fusion.18 = f32[512,3584]{1,0:T(8,128)} fusion(bf16[512,896]{1,0:T(8,128)(2,1)} %reshape_reshape.3, bf16[896,3584]{1,0:T(8,128)(2,1)} %param.13), kind=kOutput, calls=%fused_computation.25 | convolution fusion | flops 3288334336 | bytes 14680064 | tf_op jit(solution)/shard_map/dot_general | solution.py:38
  116.4 0.0 reduce-scatter.2.cloned.1.call-update
  116.5 0.0 copy-done.1
  116.5 0.1 iota_compare_fusion.1
  116.5 67.4 %reduce-scatter.2.cloned.1.call-done = f32[512,896]{1,0:T(8,128)} async-done(((f32[512,3584]{1,0:T(8,128)}), f32[512,896]{1,0:T(8,128)}) %reduce-scatter.2.cloned.1.call-update) | async-done | bytes 1835024 | tf_op jit(solution)/shard_map/reduce_scatter | solution.py:39
  184.0 2.0 select_convert_fusion
  186.0 0.1 fusion.15
  186.0 1.5 collective-permute-start.2
  187.6 3.3 %collective-permute-start.3 = (bf16[2,128,896]{2,1,0:T(8,128)(2,1)S(1)}, bf16[2,128,896]{2,1,0:T(8,128)(2,1)S(1)}, u32[]{:S(2)}, u32[]{:S(2)}) collective-permute-start(bf16[2,128,896]{2,1,0:T(8,128)(2,1)S(1)} %get-tuple-element.6), channel_id=1, source_target_pairs={{0,28},{4,0},{8,4},{12,8},{16,12},{20,16},{24,20},{28,24},{1,29},{... | collective-permute-start | bytes 1376264 | tf_op jit(solution)/shard_map/ppermute | solution.py:13
  190.8 0.0 collective-permute-start
  190.8 4.7 %collective-permute-start.1 = (s32[1]{0:T(128)}, s32[1]{0:T(128)}, u32[]{:S(2)}, u32[]{:S(2)}) collective-permute-start(s32[1]{0:T(128)} %param.16), channel_id=1, source_target_pairs={{0,28},{4,0},{8,4},{12,8},{16,12},{20,16},{24,20},{28,24},{1,29},{... | collective-permute-start | bytes 20 | tf_op jit(solution)/shard_map/ppermute | solution.py:13
  196.8 10.2 %collective-permute-done = s32[1]{0:T(128)} collective-permute-done((s32[1]{0:T(128)}, s32[1]{0:T(128)}, u32[]{:S(2)}, u32[]{:S(2)}) %collective-permute-start) | collective-permute-done | bytes 36 | tf_op jit(solution)/shard_map/ppermute | solution.py:13
  207.1 2.3 %collective-permute-done.1 = s32[1]{0:T(128)} collective-permute-done((s32[1]{0:T(128)}, s32[1]{0:T(128)}, u32[]{:S(2)}, u32[]{:S(2)}) %collective-permute-start.1) | collective-permute-done | bytes 36 | tf_op jit(solution)/shard_map/ppermute | solution.py:13
  209.3 1.2 select_select_fusion
  210.5 0.0 collective-permute-done.2
  210.5 0.0 collective-permute-done.3
  210.6 1.6 maximum_select_fusion
Async XLA Ops:
  6.5 3.2 %copy-start = (bf16[4,2048,128]{2,1,0:T(8,128)(2,1)S(1)}, bf16[4,2048,128]{2,1,0:T(8,128)(2,1)}, u32[]{:S(2)}) copy-start(bf16[4,2048,128]{2,1,0:T(8,128)(2,1)} %param.9) | copy-start | bytes 6291460
  6.5 177.4 %reduce-scatter.2.cloned.1.call-start = ((), (), s32[]{:S(2)}) async-start(), calls=%async_computation.1 | async-start | bytes 9175040 | tf_op jit(solution)/shard_map/reduce_scatter | solution.py:39
  64.2 52.3 %copy-start.1 = (s32[4]{0:T(128)S(1)}, s32[4]{0:T(128)}, u32[]{:S(2)}) copy-start(s32[4]{0:T(128)} %param.14) | copy-start | bytes 52
  186.0 24.5 %collective-permute-start.2 = (bf16[2,128,896]{2,1,0:T(8,128)(2,1)S(1)}, bf16[2,128,896]{2,1,0:T(8,128)(2,1)S(1)}, u32[]{:S(2)}, u32[]{:S(2)}) collective-permute-start(bf16[2,128,896]{2,1,0:T(8,128)(2,1)S(1)} %get-tuple-element.5), channel_id=1, source_target_pairs={{0,4},{4,8},{8,12},{12,16},{16,20},{20,24},{24,28},{28,0},{1,5},{5... | collective-permute-start | bytes 1376264 | tf_op jit(solution)/shard_map/ppermute | solution.py:13
  187.6 23.0 %collective-permute-start.3 = (bf16[2,128,896]{2,1,0:T(8,128)(2,1)S(1)}, bf16[2,128,896]{2,1,0:T(8,128)(2,1)S(1)}, u32[]{:S(2)}, u32[]{:S(2)}) collective-permute-start(bf16[2,128,896]{2,1,0:T(8,128)(2,1)S(1)} %get-tuple-element.6), channel_id=1, source_target_pairs={{0,28},{4,0},{8,4},{12,8},{16,12},{20,16},{24,20},{28,24},{1,29},{... | collective-permute-start | bytes 1376264 | tf_op jit(solution)/shard_map/ppermute | solution.py:13
  190.8 16.2 %collective-permute-start = (s32[1]{0:T(128)}, s32[1]{0:T(128)}, u32[]{:S(2)}, u32[]{:S(2)}) collective-permute-start(s32[1]{0:T(128)} %param.17), channel_id=1, source_target_pairs={{0,4},{4,8},{8,12},{12,16},{16,20},{20,24},{24,28},{28,0},{1,5},{5... | collective-permute-start | bytes 20 | tf_op jit(solution)/shard_map/ppermute | solution.py:13
  190.8 18.5 %collective-permute-start.1 = (s32[1]{0:T(128)}, s32[1]{0:T(128)}, u32[]{:S(2)}, u32[]{:S(2)}) collective-permute-start(s32[1]{0:T(128)} %param.16), channel_id=1, source_target_pairs={{0,28},{4,0},{8,4},{12,8},{16,12},{20,16},{24,20},{28,24},{1,29},{... | collective-permute-start | bytes 20 | tf_op jit(solution)/shard_map/ppermute | solution.py:13
Sparse Core Ops, SparseCore 0:
  116.6 67.3 reduce-scatter.1
where the time goes:
time: 219 us
  waiting for transfers between devices  79.9 us (36%)
  matrix products  62.1 us (28%)
  other arithmetic  48.3 us (22%)
  between operations  14.8 us (7%)
  starting transfers between devices  9.5 us (4%)
  local copies, waits for them, and re-layouts  4.4 us (2%)
    reduce_scatter x1, waiting for transfers between devices, finish(): lax.psum_scatter(partial_value, 'tp', scatter_dimension=1, tiled=True)  67.4 us
    sub x1, other arithmetic, attend(): weights_exp = jnp.where(inside, jnp.exp(scores - row_max), jnp.float32(0.0))  42.8 us
    dot_general x1, matrix products, attend(): jnp.einsum('srp,spd->srd', weights, value_rows, preferred_element_type=jn...  40.3 us
    ppermute x4, waiting for transfers between devices, passed_along(): return lax.ppermute(value, axis, pairs)  12.5 us
    dot_general x1, matrix products, attend(): jnp.einsum('srd,spd->srp', flat_rows, key_rows, preferred_element_type=jn...  11.7 us
    dot_general x1, matrix products, finish(): jnp.dot(flat_attn, out_weight, preferred_element_type=jnp.float32)  10.1 us
    ppermute x4, starting transfers between devices, passed_along(): return lax.ppermute(value, axis, pairs)  9.5 us
  transfers between devices with their start and end apart: 5, of which 3 were waited for; matrix products, arithmetic and copies ran while one was open for 1% of the time, Pallas kernels for 0%

commit v1 on v0

v1 whole, which is shorter than its diff:
```python
import functools

import jax
import jax.numpy as jnp
from jax import lax
from jax.experimental import pallas as pl
from jax.experimental.pallas import tpu as pltpu
from jax.sharding import PartitionSpec as P

TILE = 128
S_MAX = 2
GROUP = 32
SEG = 512
LOG2E = 1.4426950408889634
MASKED = -1e30


def block_kernel(
    live_ref, shard_ref, q_ref, k_ref, v_ref, tiles_ref, w_hbm,
    send_ref, keep_ref,
    w_ref, kx_ref, vx_ref, qx_ref, s_ref, mx_ref, acc_ref, attn_ref, w_sem,
):
    block = shard_ref[4]
    w_copy = pltpu.make_async_copy(w_hbm, w_ref, w_sem)
    w_copy.start()
    nodes, width = q_ref.shape[1], q_ref.shape[2]
    hd = k_ref.shape[2]
    heads = width // hd
    places = k_ref.shape[1]
    shard_cols = send_ref.shape[2]
    scale = jnp.float32(hd**-0.5 * LOG2E)
    live = live_ref[block]

    kx_ref[:, :hd] = k_ref[0]
    tile_of = lax.broadcasted_iota(jnp.int32, (places, hd), 0) // TILE
    lane_of = lax.broadcasted_iota(jnp.int32, (places, hd), 1)
    kx_ref[:, hd:] = jnp.where(tile_of == lane_of, 1.0, 0.0).astype(jnp.bfloat16)
    vx_ref[:, :hd] = v_ref[0]
    vx_ref[:, hd:] = jnp.ones((places, hd), jnp.bfloat16)

    sub = lax.broadcasted_iota(jnp.int32, (nodes, nodes), 0)
    lane = lax.broadcasted_iota(jnp.int32, (nodes, nodes), 1)
    tiles_row = jnp.broadcast_to(tiles_ref[pl.ds(block, 1), :], (nodes, nodes))
    reach_row = jnp.where(lane < live, tiles_row, 0)
    key_row = (reach_row * nodes + (nodes - 1 - lane)).astype(jnp.float32)
    key_col = key_row.T
    above = jnp.where(key_col > key_row, 1.0, 0.0)
    rank_row = jnp.sum(above, axis=0, keepdims=True)
    below = jnp.where(key_row > key_col, 1.0, 0.0)
    rank_col = jnp.sum(below, axis=1, keepdims=True)
    to_sorted = rank_row == sub.astype(jnp.float32)
    to_nodes = jnp.where(rank_col == lane.astype(jnp.float32), 1.0, 0.0).astype(jnp.bfloat16)
    reach_sorted = jnp.sum(
        jnp.where(to_sorted, reach_row.astype(jnp.float32), 0.0), axis=1, keepdims=True
    )
    to_sorted = jnp.where(to_sorted, 1.0, 0.0).astype(jnp.bfloat16)
    q_sorted = jnp.dot(to_sorted, q_ref[0], preferred_element_type=jnp.float32).astype(jnp.bfloat16)
    seen = jnp.maximum(reach_sorted, 1.0)
    bias = jnp.where(lax.broadcasted_iota(jnp.int32, (nodes, hd), 1).astype(jnp.float32) < seen, 0.0, MASKED)
    bias = jnp.where(lax.broadcasted_iota(jnp.int32, (nodes, hd), 1) < places // TILE, bias, 0.0)
    bias = bias.astype(jnp.bfloat16)
    rows = heads * GROUP
    for g in range(nodes // GROUP):
        for h in range(heads):
            at = slice(g * rows + h * GROUP, g * rows + (h + 1) * GROUP)
            qx_ref[at, :hd] = q_sorted[g * GROUP : (g + 1) * GROUP, h * hd : (h + 1) * hd]
            qx_ref[at, hd:] = bias[g * GROUP : (g + 1) * GROUP]

    for g in range(nodes // GROUP):
        longest = jnp.max(reach_sorted[g * GROUP : (g + 1) * GROUP]).astype(jnp.int32)
        segs = (longest * TILE + SEG - 1) // SEG

        @pl.when(segs == 0)
        def _():
            attn_ref[g * GROUP : (g + 1) * GROUP, :] = jnp.zeros((GROUP, width), jnp.bfloat16)

        @pl.when(segs > 0)
        def _():
            mx_ref[...] = jnp.full(mx_ref.shape, MASKED, jnp.float32)
            acc_ref[...] = jnp.zeros_like(acc_ref)
            at = slice(g * rows, (g + 1) * rows)

            @pl.loop(0, segs)
            def _(i):
                places_at = pl.ds(pl.multiple_of(i * SEG, SEG), SEG)
                s = lax.dot_general(
                    qx_ref[at, :], kx_ref[places_at, :], (((1,), (1,)), ((), ())),
                    preferred_element_type=jnp.float32,
                )
                s_ref[:, places_at] = s
                m = s[:, :hd]
                for t in range(1, SEG // hd):
                    m = jnp.maximum(m, s[:, t * hd : (t + 1) * hd])
                mx_ref[...] = jnp.maximum(mx_ref[...], m)

            top = jnp.max(mx_ref[...], axis=1, keepdims=True)

            @pl.loop(0, segs)
            def _(i):
                places_at = pl.ds(pl.multiple_of(i * SEG, SEG), SEG)
                p = jnp.exp2((s_ref[:, places_at] - top) * scale).astype(jnp.bfloat16)
                acc_ref[...] += jnp.dot(p, vx_ref[places_at, :], preferred_element_type=jnp.float32)

            mixed = (acc_ref[:, :hd] / acc_ref[:, hd:]).astype(jnp.bfloat16)
            for h in range(heads):
                attn_ref[g * GROUP : (g + 1) * GROUP, h * hd : (h + 1) * hd] = mixed[
                    h * GROUP : (h + 1) * GROUP
                ]

    attn = jnp.dot(to_nodes, attn_ref[...], preferred_element_type=jnp.float32).astype(jnp.bfloat16)
    w_copy.wait()
    for s in range(4):
        cols = pl.ds(pl.multiple_of(shard_ref[s] * shard_cols, 128), shard_cols)
        part = jnp.dot(attn, w_ref[:, cols], preferred_element_type=jnp.float32).astype(jnp.bfloat16)
        if s < 2:
            send_ref[s] = part
        else:
            keep_ref[s - 2] = part


def block_partials(j, q, k, v, tiles, live, w, shards):
    blocks, nodes, width = q.shape
    places, hd = k.shape[1], k.shape[2]
    heads = width // hd
    rows = heads * GROUP
    cols = w.shape[1] // 4
    info = jnp.concatenate([shards, jnp.full((1,), j, jnp.int32)])
    out = jax.ShapeDtypeStruct((2, nodes, cols), jnp.bfloat16)
    grid_spec = pltpu.PrefetchScalarGridSpec(
        num_scalar_prefetch=2,
        grid=(1,),
        in_specs=[
            pl.BlockSpec((1, nodes, width), lambda i, *_: (j, 0, 0)),
            pl.BlockSpec((1, places, hd), lambda i, *_: (j, 0, 0)),
            pl.BlockSpec((1, places, hd), lambda i, *_: (j, 0, 0)),
            pl.BlockSpec((blocks, nodes), lambda i, *_: (0, 0)),
            pl.BlockSpec(memory_space=pl.ANY),
        ],
        out_specs=[
            pl.BlockSpec((2, nodes, cols), lambda i, *_: (0, 0, 0)),
            pl.BlockSpec((2, nodes, cols), lambda i, *_: (0, 0, 0)),
        ],
        scratch_shapes=[
            pltpu.VMEM(w.shape, jnp.bfloat16),
            pltpu.VMEM((places, 2 * hd), jnp.bfloat16),
            pltpu.VMEM((places, 2 * hd), jnp.bfloat16),
            pltpu.VMEM((heads * nodes, 2 * hd), jnp.bfloat16),
            pltpu.VMEM((rows, places), jnp.float32),
            pltpu.VMEM((rows, hd), jnp.float32),
            pltpu.VMEM((rows, 2 * hd), jnp.float32),
            pltpu.VMEM((nodes, width), jnp.bfloat16),
            pltpu.SemaphoreType.DMA,
        ],
    )
    return pl.pallas_call(
        block_kernel,
        grid_spec=grid_spec,
        out_shape=(out, out),
        compiler_params=pltpu.CompilerParams(vmem_limit_bytes=32 << 20),
        cost_estimate=pl.CostEstimate(
            flops=2 * nodes * width * (2 * places + w.shape[1]),
            bytes_accessed=w.size * 2 + 4 * places * hd,
            transcendentals=nodes * heads * places,
        ),
    )(live, info, q, k, v, tiles, w)


def on_device(
    kv_keys, kv_values, queries, hidden, out_weight, block_live, node_tiles, left_count, right_count
):
    blocks, nodes, _ = queries.shape
    tp = lax.axis_size("tp")
    ring = lax.axis_size("blk")
    me = lax.axis_index("tp")
    mine, mate = me, me ^ 1
    shards = jnp.stack([mate, mate ^ 2, mine, mine ^ 2]).astype(jnp.int32)
    to_mate = [(i, i ^ 1) for i in range(tp)]
    to_across = [(i, i ^ 2) for i in range(tp)]
    to_next = [(i, (i + 1) % ring) for i in range(ring)]
    to_prev = [(i, (i - 1) % ring) for i in range(ring)]
    left, right = left_count[0], right_count[0]
    own = [None] * blocks
    from_next = [None] * S_MAX
    from_prev = [None] * S_MAX
    zero = jnp.zeros((), jnp.bfloat16)
    for j in range(blocks):
        send, keep = block_partials(
            j, queries, kv_keys, kv_values, node_tiles, block_live, out_weight, shards
        )
        got = lax.ppermute(send, "tp", to_mate)
        across = (keep[1].astype(jnp.float32) + got[1].astype(jnp.float32)).astype(jnp.bfloat16)
        other = lax.ppermute(across, "tp", to_across)
        total = (
            keep[0].astype(jnp.float32)
            + got[0].astype(jnp.float32)
            + other.astype(jnp.float32)
            + hidden[j].astype(jnp.float32)
        )
        alive = jnp.arange(nodes, dtype=jnp.int32)[:, None] < block_live[j]
        result = jnp.where(alive, total, 0.0).astype(jnp.bfloat16)
        stays = (left <= j) & (j < blocks - right)
        own[j] = jnp.where(stays, result, zero)
        if j < S_MAX:
            from_next[j] = lax.ppermute(jnp.where(j < left, result, zero), "blk", to_prev)
        if j >= blocks - S_MAX:
            goes = blocks - j <= right
            from_prev[j - blocks + S_MAX] = lax.ppermute(
                jnp.where(goes, result, zero), "blk", to_next
            )
    return jnp.stack(from_prev + own + from_next)


def solution(mesh):
    return jax.shard_map(
        on_device,
        mesh=mesh,
        in_specs=(
            P("blk", None, "tp"),
            P("blk", None, "tp"),
            P("blk", None, "tp"),
            P("blk", None, "tp"),
            P("tp", None),
            P("blk"),
            P("blk", None),
            P("blk"),
            P("blk"),
        ),
        out_specs=P("blk", None, "tp"),
        check_vma=False,
    )
```

time: 219 us -> 110 us (0.50)
  matrix products: 62.1 us -> 0 us
  waiting for transfers between devices: 79.9 us -> 27.3 us
  other arithmetic: 48.3 us -> 7.66 us
  Pallas kernels: 0 us -> 28 us
  local copies, waits for them, and re-layouts: 4.4 us -> 25.1 us
  between operations: 14.8 us -> 1.59 us
  starting transfers between devices: 9.5 us -> 18.9 us
    reduce_scatter x1 -> x0, waiting for transfers between devices: 67.4 us -> none  [finish(): lax.psum_scatter(partial_value, 'tp', scatter_dimension=1, tiled=True)]
    dot_general x3 -> x0, matrix products: 62.1 us -> none  [the longest x1 40.3 us: attend(): jnp.einsum('srp,spd->srd', weights, value_rows, preferred_element_type=jn...]
    sub x1 -> x0, other arithmetic: 42.8 us -> none  [attend(): weights_exp = jnp.where(inside, jnp.exp(scores - row_max), jnp.float32(0.0))]
    pallas_call x0 -> x4, Pallas kernels: none -> 28 us  [block_partials(): pl.pallas_call(block_kernel, grid_spec=grid_spec, out_shape=(out, out), c...]
    unnamed x4 -> x47, local copies, waits for them, and re-layouts: 0.01 us -> 23.4 us
    ppermute x4 -> x12, waiting for transfers between devices: 12.5 us -> 27.3 us  [the longest x4 11.9 us: on_device(): other = lax.ppermute(across, 'tp', to_across)]
    ppermute x4 -> x12, starting transfers between devices: 9.5 us -> 18.9 us  [the longest x2 6.39 us: on_device(): lax.ppermute(jnp.where(j < left, result, zero), 'blk', to_prev)]
    lt x1 -> x3, other arithmetic: 0.07 us -> 2.58 us  [on_device(): alive = jnp.arange(nodes, dtype=jnp.int32)[:, None] < block_live[j]]
  transfers between devices with their start and end apart: 5 -> 12, of which waited for: 3 -> 6; matrix products, arithmetic and copies ran while one was open for 1% -> 8% of each run, Pallas kernels for 0% -> 19%
where the time goes in v1:
time: 110 us; the launch traced here: 109 us
  Pallas kernels  28 us (25%)
  waiting for transfers between devices  27.3 us (25%)
  local copies, waits for them, and re-layouts  25.1 us (23%)
  starting transfers between devices  18.9 us (17%)
  other arithmetic  7.66 us (7%)
  between operations  1.59 us (1%)
    pallas_call x4, Pallas kernels, block_partials(): pl.pallas_call(block_kernel, grid_spec=grid_spec, out_shape=(out, out), c...  28 us
    unnamed x47, local copies, waits for them, and re-layouts  23.4 us
    ppermute x4, waiting for transfers between devices, on_device(): other = lax.ppermute(across, 'tp', to_across)  11.9 us
    ppermute x2, waiting for transfers between devices, on_device(): lax.ppermute(jnp.where(goes, result, zero), 'blk', to_next)  11.4 us
    ppermute x2, starting transfers between devices, on_device(): lax.ppermute(jnp.where(j < left, result, zero), 'blk', to_prev)  6.39 us
    ppermute x2, starting transfers between devices, on_device(): lax.ppermute(jnp.where(goes, result, zero), 'blk', to_next)  6.14 us
    ppermute x4, starting transfers between devices, on_device(): other = lax.ppermute(across, 'tp', to_across)  5.22 us
    ppermute x2, waiting for transfers between devices, on_device(): lax.ppermute(jnp.where(j < left, result, zero), 'blk', to_prev)  3.86 us
  transfers between devices with their start and end apart: 12, of which 6 were waited for; matrix products, arithmetic and copies ran while one was open for 8% of the time, Pallas kernels for 19%

profile of v1, /device:TPU:0, one launch (start us, length us, event | category | flops | bytes accessed | tf_op | source)
XLA Modules:
  0.0 108.5 jit_solution(16930578817358680665)
XLA Ops:
  0.0 0.1 concatenate.16.shard_ref
  0.1 2.8 %copy-done = bf16[896,3584]{1,0:T(8,128)(2,1)S(1)} copy-done((bf16[896,3584]{1,0:T(8,128)(2,1)S(1)}, bf16[896,3584]{1,0:T(8,128)(2,1)}, u32[]{:S(2)}) %copy-start) | copy-done | bytes 6422552
  2.9 1.6 %copy-done.4 = bf16[4,2048,128]{2,1,0:T(8,128)(2,1)S(1)} copy-done((bf16[4,2048,128]{2,1,0:T(8,128)(2,1)S(1)}, bf16[4,2048,128]{2,1,0:T(8,128)(2,1)}, u32[]{:S(2)}) %copy-start.4) | copy-done | bytes 2097176
  4.5 1.6 %copy-done.6 = bf16[4,2048,128]{2,1,0:T(8,128)(2,1)S(1)} copy-done((bf16[4,2048,128]{2,1,0:T(8,128)(2,1)S(1)}, bf16[4,2048,128]{2,1,0:T(8,128)(2,1)}, u32[]{:S(2)}) %copy-start.6) | copy-done | bytes 2097176
  6.1 1.2 %copy-done.10 = bf16[4,128,896]{2,1,0:T(8,128)(2,1)S(1)} copy-done((bf16[4,128,896]{2,1,0:T(8,128)(2,1)S(1)}, bf16[4,128,896]{2,1,0:T(8,128)(2,1)}, u32[]{:S(2)}) %copy-start.10) | copy-done | bytes 917528
  7.3 0.7 copy-done.16
  8.0 0.7 copy-done.18
  8.6 7.5 %shard_map.91 = (bf16[2,128,896]{2,1,0:T(8,128)(2,1)}, bf16[2,128,896]{2,1,0:T(8,128)(2,1)S(1)}) custom-call(s32[4]{0:T(128)S(1)} %copy-done.18, s32[5]{0:T(128)S(1)} %concatenate.16.shard_ref, bf16[4,128,896]{2,1,0:T(8,128)(2,1)S(1)} %copy-done.10, bf16[4,2048,128]{2,1,0:T(8,128)(2,1)S(1)} %copy-done.4, bf16[4,2048,128]{2,1,0:T(8,128)(2,1)S(1)} %copy-done.6, ...), custom_call_target="tpu_custom_call" | custom-call | flops 1761607680 | bytes 7471104 | tf_op jit(solution)/shard_map/pallas_call | solution.py:155
  16.2 0.6 collective-permute-start
  16.7 0.1 concatenate.17.shard_ref
  16.8 2.8 %copy-done.1 = bf16[896,3584]{1,0:T(8,128)(2,1)S(1)} copy-done((bf16[896,3584]{1,0:T(8,128)(2,1)S(1)}, bf16[896,3584]{1,0:T(8,128)(2,1)}, u32[]{:S(2)}) %copy-start.1) | copy-done | bytes 6422552
  19.7 1.6 %copy-done.7 = bf16[4,2048,128]{2,1,0:T(8,128)(2,1)S(1)} copy-done((bf16[4,2048,128]{2,1,0:T(8,128)(2,1)S(1)}, bf16[4,2048,128]{2,1,0:T(8,128)(2,1)}, u32[]{:S(2)}) %copy-start.7) | copy-done | bytes 2097176
  21.2 6.5 %shard_map.92 = (bf16[2,128,896]{2,1,0:T(8,128)(2,1)}, bf16[2,128,896]{2,1,0:T(8,128)(2,1)S(1)}) custom-call(s32[4]{0:T(128)S(1)} %copy-done.19, s32[5]{0:T(128)S(1)} %concatenate.17.shard_ref, bf16[4,128,896]{2,1,0:T(8,128)(2,1)S(1)} %copy-done.11, bf16[4,2048,128]{2,1,0:T(8,128)(2,1)S(1)} %copy-done.5, bf16[4,2048,128]{2,1,0:T(8,128)(2,1)S(1)} %copy-done.7, ...), custom_call_target="tpu_custom_call" | custom-call | flops 1761607680 | bytes 7471104 | tf_op jit(solution)/shard_map/pallas_call | solution.py:155
  27.8 0.8 copy-done.12
  28.6 0.1 concatenate.19.shard_ref
  28.7 2.8 %copy-done.2 = bf16[896,3584]{1,0:T(8,128)(2,1)S(1)} copy-done((bf16[896,3584]{1,0:T(8,128)(2,1)S(1)}, bf16[896,3584]{1,0:T(8,128)(2,1)}, u32[]{:S(2)}) %copy-start.2) | copy-done | bytes 6422552
  31.5 1.6 %copy-done.8 = bf16[4,2048,128]{2,1,0:T(8,128)(2,1)S(1)} copy-done((bf16[4,2048,128]{2,1,0:T(8,128)(2,1)S(1)}, bf16[4,2048,128]{2,1,0:T(8,128)(2,1)}, u32[]{:S(2)}) %copy-start.8) | copy-done | bytes 2097176
  33.1 5.9 %shard_map.94 = (bf16[2,128,896]{2,1,0:T(8,128)(2,1)}, bf16[2,128,896]{2,1,0:T(8,128)(2,1)S(1)}) custom-call(s32[4]{0:T(128)S(1)} %copy-done.19, s32[5]{0:T(128)S(1)} %concatenate.19.shard_ref, bf16[4,128,896]{2,1,0:T(8,128)(2,1)S(1)} %copy-done.11, bf16[4,2048,128]{2,1,0:T(8,128)(2,1)S(1)} %copy-done.5, bf16[4,2048,128]{2,1,0:T(8,128)(2,1)S(1)} %copy-done.8, ...), custom_call_target="tpu_custom_call" | custom-call | flops 1761607680 | bytes 7471104 | tf_op jit(solution)/shard_map/pallas_call | solution.py:155
  39.0 0.8 copy-done.14
  39.8 0.5 collective-permute-start.8
  40.3 0.1 concatenate.18.shard_ref
  40.4 2.8 %copy-done.3 = bf16[896,3584]{1,0:T(8,128)(2,1)S(1)} copy-done((bf16[896,3584]{1,0:T(8,128)(2,1)S(1)}, bf16[896,3584]{1,0:T(8,128)(2,1)}, u32[]{:S(2)}) %copy-start.3) | copy-done | bytes 6422552
  43.2 1.6 %copy-done.9 = bf16[4,2048,128]{2,1,0:T(8,128)(2,1)S(1)} copy-done((bf16[4,2048,128]{2,1,0:T(8,128)(2,1)S(1)}, bf16[4,2048,128]{2,1,0:T(8,128)(2,1)}, u32[]{:S(2)}) %copy-start.9) | copy-done | bytes 2097176
  44.8 8.0 %shard_map.93 = (bf16[2,128,896]{2,1,0:T(8,128)(2,1)S(1)}, bf16[2,128,896]{2,1,0:T(8,128)(2,1)S(1)}) custom-call(s32[4]{0:T(128)S(1)} %copy-done.19, s32[5]{0:T(128)S(1)} %concatenate.18.shard_ref, bf16[4,128,896]{2,1,0:T(8,128)(2,1)S(1)} %copy-done.11, bf16[4,2048,128]{2,1,0:T(8,128)(2,1)S(1)} %copy-done.5, bf16[4,2048,128]{2,1,0:T(8,128)(2,1)S(1)} %copy-done.9, ...), custom_call_target="tpu_custom_call" | custom-call | flops 1761607680 | bytes 7471104 | tf_op jit(solution)/shard_map/pallas_call | solution.py:155
  52.8 0.1 collective-permute-start.6
  54.3 0.7 fusion.16
  55.0 0.6 iota_compare_fusion.3
  55.6 0.6 iota_compare_fusion.1
  56.3 1.3 %iota_compare_fusion = (pred[128]{0:T(512)(128)(4,1)S(1)}, pred[128]{0:T(512)(128)(4,1)S(1)}) fusion(s32[]{:T(128)} %bitcast.23, s32[]{:T(128)} %bitcast.11), kind=kLoop, calls=%fused_computation.36 | loop fusion | flops 256 | bytes 264 | tf_op jit(solution)/shard_map/lt | solution.py:199
  57.6 1.0 fusion.8
  58.6 3.0 %collective-permute-start.1 = (bf16[128,896]{1,0:T(8,128)(2,1)S(1)}, bf16[128,896]{1,0:T(8,128)(2,1)S(1)}, u32[]{:S(2)}, u32[]{:S(2)}) collective-permute-start(bf16[128,896]{1,0:T(8,128)(2,1)S(1)} %fusion.8), channel_id=1, source_target_pairs={{0,2},{1,3},{2,0},{3,1},{4,6},{5,7},{6,4},{7,5},{8,10},{9,11},{10,... | collective-permute-start | bytes 688136 | tf_op jit(solution)/shard_map/ppermute | solution.py:192
  61.6 1.0 fusion.9
  62.6 0.1 collective-permute-start.4
  62.7 1.0 fusion.11
  63.7 2.1 %collective-permute-start.9 = (bf16[128,896]{1,0:T(8,128)(2,1)S(1)}, bf16[128,896]{1,0:T(8,128)(2,1)S(1)}, u32[]{:S(2)}, u32[]{:S(2)}) collective-permute-start(bf16[128,896]{1,0:T(8,128)(2,1)S(1)} %fusion.11), channel_id=1, source_target_pairs={{0,2},{1,3},{2,0},{3,1},{4,6},{5,7},{6,4},{7,5},{8,10},{9,11},{10,... | collective-permute-start | bytes 688136 | tf_op jit(solution)/shard_map/ppermute | solution.py:192
  65.8 0.1 collective-permute-start.7
  65.9 2.1 %collective-permute-done.1 = bf16[128,896]{1,0:T(8,128)(2,1)S(1)} collective-permute-done((bf16[128,896]{1,0:T(8,128)(2,1)S(1)}, bf16[128,896]{1,0:T(8,128)(2,1)S(1)}, u32[]{:S(2)}, u32[]{:S(2)}) %collective-permute-start.1) | collective-permute-done | bytes 229408 | tf_op jit(solution)/shard_map/ppermute | solution.py:192
  68.0 4.9 %collective-permute-done.4 = bf16[128,896]{1,0:T(8,128)(2,1)S(1)} collective-permute-done((bf16[128,896]{1,0:T(8,128)(2,1)S(1)}, bf16[128,896]{1,0:T(8,128)(2,1)S(1)}, u32[]{:S(2)}, u32[]{:S(2)}) %collective-permute-start.4) | collective-permute-done | bytes 229408 | tf_op jit(solution)/shard_map/ppermute | solution.py:192
  72.9 4.9 %collective-permute-done.9 = bf16[128,896]{1,0:T(8,128)(2,1)S(1)} collective-permute-done((bf16[128,896]{1,0:T(8,128)(2,1)S(1)}, bf16[128,896]{1,0:T(8,128)(2,1)S(1)}, u32[]{:S(2)}, u32[]{:S(2)}) %collective-permute-start.9) | collective-permute-done | bytes 229408 | tf_op jit(solution)/shard_map/ppermute | solution.py:192
  77.8 1.6 %broadcast_select_fusion = (bf16[128,896]{1,0:T(8,128)(2,1)S(1)}, bf16[128,896]{1,0:T(8,128)(2,1)S(1)}, bf16[128,896]{1,0:T(8,128)(2,1)S(1)}, bf16[128,896]{1,0:...) fusion(pred[]{:T(512)} %bitcast.34, bf16[4,128,896]{2,1,0:T(8,128)(2,1)S(1)} %copy-done.20, ...), kind=kLoop, calls=%fused_computation.32 | loop fusion | flops 3440640 | bytes 4129155 | tf_op jit(solution)/shard_map/jit(_where)/select_n | solution.py:204
  79.5 6.1 %collective-permute-start.2 = (bf16[128,896]{1,0:T(8,128)(2,1)S(1)}, bf16[128,896]{1,0:T(8,128)(2,1)S(1)}, u32[]{:S(2)}, u32[]{:S(2)}) collective-permute-start(bf16[128,896]{1,0:T(8,128)(2,1)S(1)} %get-tuple-element.31), channel_id=1, source_target_pairs={{0,4},{4,8},{8,12},{12,16},{16,20},{20,24},{24,28},{28,0},{1,5},{5... | collective-permute-start | bytes 688136 | tf_op jit(solution)/shard_map/ppermute | solution.py:207
  85.6 0.1 collective-permute-start.5
  85.6 0.2 broadcast_select_fusion.1
  85.8 6.3 %collective-permute-start.10 = (bf16[128,896]{1,0:T(8,128)(2,1)S(1)}, bf16[128,896]{1,0:T(8,128)(2,1)S(1)}, u32[]{:S(2)}, u32[]{:S(2)}) collective-permute-start(bf16[128,896]{1,0:T(8,128)(2,1)S(1)} %get-tuple-element.23), channel_id=1, source_target_pairs={{0,28},{4,0},{8,4},{12,8},{16,12},{20,16},{24,20},{28,24},{1,29},{... | collective-permute-start | bytes 688136 | tf_op jit(solution)/shard_map/ppermute | solution.py:204
  92.2 9.0 %collective-permute-done.2 = bf16[128,896]{1,0:T(8,128)(2,1)S(1)} collective-permute-done((bf16[128,896]{1,0:T(8,128)(2,1)S(1)}, bf16[128,896]{1,0:T(8,128)(2,1)S(1)}, u32[]{:S(2)}, u32[]{:S(2)}) %collective-permute-start.2) | collective-permute-done | bytes 229408 | tf_op jit(solution)/shard_map/ppermute | solution.py:207
  101.2 2.4 %collective-permute-done.5 = bf16[128,896]{1,0:T(8,128)(2,1)S(1)} collective-permute-done((bf16[128,896]{1,0:T(8,128)(2,1)S(1)}, bf16[128,896]{1,0:T(8,128)(2,1)S(1)}, u32[]{:S(2)}, u32[]{:S(2)}) %collective-permute-start.5) | collective-permute-done | bytes 229408 | tf_op jit(solution)/shard_map/ppermute | solution.py:207
  104.0 3.9 %collective-permute-done.11 = bf16[128,896]{1,0:T(8,128)(2,1)S(1)} collective-permute-done((bf16[128,896]{1,0:T(8,128)(2,1)S(1)}, bf16[128,896]{1,0:T(8,128)(2,1)S(1)}, u32[]{:S(2)}, u32[]{:S(2)}) %collective-permute-start.11) | collective-permute-done | bytes 229408 | tf_op jit(solution)/shard_map/ppermute | solution.py:204
  107.8 0.7 bitcast_dynamic-update-slice_fusion
  (46 shorter events, 0.5 us)
Async XLA Ops:
  0.1 2.8 %copy-start = (bf16[896,3584]{1,0:T(8,128)(2,1)S(1)}, bf16[896,3584]{1,0:T(8,128)(2,1)}, u32[]{:S(2)}) copy-start(bf16[896,3584]{1,0:T(8,128)(2,1)} %w_hbm.7) | copy-start | bytes 19267588
  2.9 1.6 %copy-start.4 = (bf16[4,2048,128]{2,1,0:T(8,128)(2,1)S(1)}, bf16[4,2048,128]{2,1,0:T(8,128)(2,1)}, u32[]{:S(2)}) copy-start(bf16[4,2048,128]{2,1,0:T(8,128)(2,1)} %k_ref.7) | copy-start | bytes 6291460
  4.5 1.6 %copy-start.6 = (bf16[4,2048,128]{2,1,0:T(8,128)(2,1)S(1)}, bf16[4,2048,128]{2,1,0:T(8,128)(2,1)}, u32[]{:S(2)}) copy-start(bf16[4,2048,128]{2,1,0:T(8,128)(2,1)} %v_ref.7) | copy-start | bytes 6291460
  6.1 1.2 %copy-start.10 = (bf16[4,128,896]{2,1,0:T(8,128)(2,1)S(1)}, bf16[4,128,896]{2,1,0:T(8,128)(2,1)}, u32[]{:S(2)}) copy-start(bf16[4,128,896]{2,1,0:T(8,128)(2,1)} %q_ref.7) | copy-start | bytes 2752516
  7.3 0.7 copy-start.16
  8.0 0.7 copy-start.18
  8.6 8.2 %copy-start.5 = (bf16[4,2048,128]{2,1,0:T(8,128)(2,1)S(1)}, bf16[4,2048,128]{2,1,0:T(8,128)(2,1)}, u32[]{:S(2)}) copy-start(bf16[4,2048,128]{2,1,0:T(8,128)(2,1)} %k_ref.7) | copy-start | bytes 6291460
  8.6 8.2 %copy-start.11 = (bf16[4,128,896]{2,1,0:T(8,128)(2,1)S(1)}, bf16[4,128,896]{2,1,0:T(8,128)(2,1)}, u32[]{:S(2)}) copy-start(bf16[4,128,896]{2,1,0:T(8,128)(2,1)} %q_ref.7) | copy-start | bytes 2752516
  8.6 8.2 %copy-start.17 = (s32[4,128]{1,0:T(4,128)S(1)}, s32[4,128]{1,0:T(4,128)}, u32[]{:S(2)}) copy-start(s32[4,128]{1,0:T(4,128)} %tiles_ref.7) | copy-start | bytes 6148
  8.6 8.2 %copy-start.19 = (s32[4]{0:T(128)S(1)}, s32[4]{0:T(128)}, u32[]{:S(2)}) copy-start(s32[4]{0:T(128)} %live_ref.7) | copy-start | bytes 52
  16.2 41.4 %collective-permute-start = (bf16[2,128,896]{2,1,0:T(8,128)(2,1)}, bf16[2,128,896]{2,1,0:T(8,128)(2,1)}, u32[]{:S(2)}, u32[]{:S(2)}) collective-permute-start(bf16[2,128,896]{2,1,0:T(8,128)(2,1)} %get-tuple-element.14), channel_id=1, source_target_pairs={{0,1},{1,0},{2,3},{3,2},{4,5},{5,4},{6,7},{7,6},{8,9},{9,8},{10,11... | collective-permute-start | bytes 1376264 | tf_op jit(solution)/shard_map/ppermute | solution.py:190
  16.8 2.8 %copy-start.1 = (bf16[896,3584]{1,0:T(8,128)(2,1)S(1)}, bf16[896,3584]{1,0:T(8,128)(2,1)}, u32[]{:S(2)}) copy-start(bf16[896,3584]{1,0:T(8,128)(2,1)} %w_hbm.7) | copy-start | bytes 19267588
  19.7 1.6 %copy-start.7 = (bf16[4,2048,128]{2,1,0:T(8,128)(2,1)S(1)}, bf16[4,2048,128]{2,1,0:T(8,128)(2,1)}, u32[]{:S(2)}) copy-start(bf16[4,2048,128]{2,1,0:T(8,128)(2,1)} %v_ref.7) | copy-start | bytes 6291460
  27.8 0.8 copy-start.12
  28.6 33.0 %collective-permute-start.3 = (bf16[2,128,896]{2,1,0:T(8,128)(2,1)}, bf16[2,128,896]{2,1,0:T(8,128)(2,1)}, u32[]{:S(2)}, u32[]{:S(2)}) collective-permute-start(bf16[2,128,896]{2,1,0:T(8,128)(2,1)} %get-tuple-element.16), channel_id=1, source_target_pairs={{0,1},{1,0},{2,3},{3,2},{4,5},{5,4},{6,7},{7,6},{8,9},{9,8},{10,11... | collective-permute-start | bytes 1376264 | tf_op jit(solution)/shard_map/ppermute | solution.py:190
  28.7 2.8 %copy-start.2 = (bf16[896,3584]{1,0:T(8,128)(2,1)S(1)}, bf16[896,3584]{1,0:T(8,128)(2,1)}, u32[]{:S(2)}) copy-start(bf16[896,3584]{1,0:T(8,128)(2,1)} %w_hbm.7) | copy-start | bytes 19267588
  31.5 1.6 %copy-start.8 = (bf16[4,2048,128]{2,1,0:T(8,128)(2,1)S(1)}, bf16[4,2048,128]{2,1,0:T(8,128)(2,1)}, u32[]{:S(2)}) copy-start(bf16[4,2048,128]{2,1,0:T(8,128)(2,1)} %v_ref.7) | copy-start | bytes 6291460
  39.0 0.8 copy-start.14
  39.8 22.8 %collective-permute-start.8 = (bf16[2,128,896]{2,1,0:T(8,128)(2,1)}, bf16[2,128,896]{2,1,0:T(8,128)(2,1)}, u32[]{:S(2)}, u32[]{:S(2)}) collective-permute-start(bf16[2,128,896]{2,1,0:T(8,128)(2,1)} %get-tuple-element.20), channel_id=1, source_target_pairs={{0,1},{1,0},{2,3},{3,2},{4,5},{5,4},{6,7},{7,6},{8,9},{9,8},{10,11... | collective-permute-start | bytes 1376264 | tf_op jit(solution)/shard_map/ppermute | solution.py:190
  40.4 2.8 %copy-start.3 = (bf16[896,3584]{1,0:T(8,128)(2,1)S(1)}, bf16[896,3584]{1,0:T(8,128)(2,1)}, u32[]{:S(2)}) copy-start(bf16[896,3584]{1,0:T(8,128)(2,1)} %w_hbm.7) | copy-start | bytes 19267588
  43.2 1.6 %copy-start.9 = (bf16[4,2048,128]{2,1,0:T(8,128)(2,1)S(1)}, bf16[4,2048,128]{2,1,0:T(8,128)(2,1)}, u32[]{:S(2)}) copy-start(bf16[4,2048,128]{2,1,0:T(8,128)(2,1)} %v_ref.7) | copy-start | bytes 6291460
  44.8 16.8 %copy-start.13 = (bf16[2,128,896]{2,1,0:T(8,128)(2,1)S(1)}, bf16[2,128,896]{2,1,0:T(8,128)(2,1)}, u32[]{:S(2)}) copy-start(bf16[2,128,896]{2,1,0:T(8,128)(2,1)} %copy-done.12) | copy-start | bytes 1376260
  44.8 17.9 %copy-start.15 = (bf16[2,128,896]{2,1,0:T(8,128)(2,1)S(1)}, bf16[2,128,896]{2,1,0:T(8,128)(2,1)}, u32[]{:S(2)}) copy-start(bf16[2,128,896]{2,1,0:T(8,128)(2,1)} %copy-done.14) | copy-start | bytes 1376260
  52.8 25.0 %copy-start.20 = (bf16[4,128,896]{2,1,0:T(8,128)(2,1)S(1)}, bf16[4,128,896]{2,1,0:T(8,128)(2,1)}, u32[]{:S(2)}) copy-start(bf16[4,128,896]{2,1,0:T(8,128)(2,1)} %param.12) | copy-start | bytes 2752516
  52.8 12.9 %collective-permute-start.6 = (bf16[2,128,896]{2,1,0:T(8,128)(2,1)S(1)}, bf16[2,128,896]{2,1,0:T(8,128)(2,1)S(1)}, u32[]{:S(2)}, u32[]{:S(2)}) collective-permute-start(bf16[2,128,896]{2,1,0:T(8,128)(2,1)S(1)} %get-tuple-element.18), channel_id=1, source_target_pairs={{0,1},{1,0},{2,3},{3,2},{4,5},{5,4},{6,7},{7,6},{8,9},{9,8},{10,11... | collective-permute-start | bytes 1376264 | tf_op jit(solution)/shard_map/ppermute | solution.py:190
  58.6 9.4 %collective-permute-start.1 = (bf16[128,896]{1,0:T(8,128)(2,1)S(1)}, bf16[128,896]{1,0:T(8,128)(2,1)S(1)}, u32[]{:S(2)}, u32[]{:S(2)}) collective-permute-start(bf16[128,896]{1,0:T(8,128)(2,1)S(1)} %fusion.8), channel_id=1, source_target_pairs={{0,2},{1,3},{2,0},{3,1},{4,6},{5,7},{6,4},{7,5},{8,10},{9,11},{10,... | collective-permute-start | bytes 688136 | tf_op jit(solution)/shard_map/ppermute | solution.py:192
  62.6 10.3 %collective-permute-start.4 = (bf16[128,896]{1,0:T(8,128)(2,1)S(1)}, bf16[128,896]{1,0:T(8,128)(2,1)S(1)}, u32[]{:S(2)}, u32[]{:S(2)}) collective-permute-start(bf16[128,896]{1,0:T(8,128)(2,1)S(1)} %fusion.9), channel_id=1, source_target_pairs={{0,2},{1,3},{2,0},{3,1},{4,6},{5,7},{6,4},{7,5},{8,10},{9,11},{10,... | collective-permute-start | bytes 688136 | tf_op jit(solution)/shard_map/ppermute | solution.py:192
  63.7 14.2 %collective-permute-start.9 = (bf16[128,896]{1,0:T(8,128)(2,1)S(1)}, bf16[128,896]{1,0:T(8,128)(2,1)S(1)}, u32[]{:S(2)}, u32[]{:S(2)}) collective-permute-start(bf16[128,896]{1,0:T(8,128)(2,1)S(1)} %fusion.11), channel_id=1, source_target_pairs={{0,2},{1,3},{2,0},{3,1},{4,6},{5,7},{6,4},{7,5},{8,10},{9,11},{10,... | collective-permute-start | bytes 688136 | tf_op jit(solution)/shard_map/ppermute | solution.py:192
  65.8 19.8 %collective-permute-start.7 = (bf16[128,896]{1,0:T(8,128)(2,1)S(1)}, bf16[128,896]{1,0:T(8,128)(2,1)S(1)}, u32[]{:S(2)}, u32[]{:S(2)}) collective-permute-start(bf16[128,896]{1,0:T(8,128)(2,1)S(1)} %fusion.10), channel_id=1, source_target_pairs={{0,2},{1,3},{2,0},{3,1},{4,6},{5,7},{6,4},{7,5},{8,10},{9,11},{10,... | collective-permute-start | bytes 688136 | tf_op jit(solution)/shard_map/ppermute | solution.py:192
  79.5 21.7 %collective-permute-start.2 = (bf16[128,896]{1,0:T(8,128)(2,1)S(1)}, bf16[128,896]{1,0:T(8,128)(2,1)S(1)}, u32[]{:S(2)}, u32[]{:S(2)}) collective-permute-start(bf16[128,896]{1,0:T(8,128)(2,1)S(1)} %get-tuple-element.31), channel_id=1, source_target_pairs={{0,4},{4,8},{8,12},{12,16},{16,20},{20,24},{24,28},{28,0},{1,5},{5... | collective-permute-start | bytes 688136 | tf_op jit(solution)/shard_map/ppermute | solution.py:207
  85.6 18.1 %collective-permute-start.5 = (bf16[128,896]{1,0:T(8,128)(2,1)S(1)}, bf16[128,896]{1,0:T(8,128)(2,1)S(1)}, u32[]{:S(2)}, u32[]{:S(2)}) collective-permute-start(bf16[128,896]{1,0:T(8,128)(2,1)S(1)} %get-tuple-element.29), channel_id=1, source_target_pairs={{0,4},{4,8},{8,12},{12,16},{16,20},{20,24},{24,28},{28,0},{1,5},{5... | collective-permute-start | bytes 688136 | tf_op jit(solution)/shard_map/ppermute | solution.py:207
  85.8 18.1 %collective-permute-start.10 = (bf16[128,896]{1,0:T(8,128)(2,1)S(1)}, bf16[128,896]{1,0:T(8,128)(2,1)S(1)}, u32[]{:S(2)}, u32[]{:S(2)}) collective-permute-start(bf16[128,896]{1,0:T(8,128)(2,1)S(1)} %get-tuple-element.23), channel_id=1, source_target_pairs={{0,28},{4,0},{8,4},{12,8},{16,12},{20,16},{24,20},{28,24},{1,29},{... | collective-permute-start | bytes 688136 | tf_op jit(solution)/shard_map/ppermute | solution.py:204
  92.1 15.7 %collective-permute-start.11 = (bf16[128,896]{1,0:T(8,128)(2,1)S(1)}, bf16[128,896]{1,0:T(8,128)(2,1)S(1)}, u32[]{:S(2)}, u32[]{:S(2)}) collective-permute-start(bf16[128,896]{1,0:T(8,128)(2,1)S(1)} %get-tuple-element.21), channel_id=1, source_target_pairs={{0,28},{4,0},{8,4},{12,8},{16,12},{20,16},{24,20},{28,24},{1,29},{... | collective-permute-start | bytes 688136 | tf_op jit(solution)/shard_map/ppermute | solution.py:204
  104.0 3.9 %copy-start.21 = (bf16[8,128,896]{2,1,0:T(8,128)(2,1)}, bf16[8,128,896]{2,1,0:T(8,128)(2,1)S(1)}, u32[]{:S(2)}) copy-start(bf16[8,128,896]{2,1,0:T(8,128)(2,1)S(1)} %bitcast_dynamic-update-slice_fusion.1) | copy-start | bytes 5505028

commit v2 on v0

v2 whole, which is shorter than its diff:
```python
import functools

import jax
import jax.numpy as jnp
from jax import lax
from jax.experimental import pallas as pl
from jax.experimental.pallas import tpu as pltpu
from jax.sharding import PartitionSpec as P


TILE = 128
S_MAX = 2
GROUP = 64
SEG = 512
LOG2E = 1.4426950408889634
MASKED = -1e30
VMEM_LIMIT = 60 << 20
CHUNKS = ((0, 2), (2, 2))


def group_softmax(n, qg, kx_ref, vx_ref, b, scale, hd):
    tops, outs = [], []
    for i in range(n):
        at = slice(i * SEG, (i + 1) * SEG)
        s = lax.dot_general(
            qg, kx_ref[b, at, :], (((1,), (1,)), ((), ())), preferred_element_type=jnp.float32
        )
        top = jnp.max(s, axis=1, keepdims=True)
        p = jnp.exp2((s - top) * scale).astype(jnp.bfloat16)
        tops.append(top)
        outs.append(jnp.dot(p, vx_ref[b, at, :], preferred_element_type=jnp.float32))
    if n == 1:
        acc = outs[0]
    else:
        top = functools.reduce(jnp.maximum, tops)
        acc = sum(o * jnp.exp2((t - top) * scale) for o, t in zip(outs, tops))
    return (acc[:, :hd] / acc[:, hd:]).astype(jnp.bfloat16)


def blocks_kernel(
    first, count, live_ref, q_hbm, k_hbm, v_hbm, hidden_hbm, tiles_hbm, w_hbm, order_hbm, *refs
):
    send_hbm, keep_hbm, mine_hbm = refs[:count], refs[count : 2 * count], refs[2 * count : 3 * count]
    (
        tiles_ref, hidden_ref, mine_ref, q_ref, w_ref, kx_ref, vx_ref, qx_ref, attn_ref, perm_ref,
        part_ref, segs_ref, sems,
    ) = refs[3 * count :]
    _, nodes, width = q_ref.shape
    places, hd = kx_ref.shape[1], kx_ref.shape[2] // 2
    heads = width // hd
    groups = nodes // GROUP
    rows = heads * GROUP
    shard_cols = part_ref.shape[2]
    scale = jnp.float32(hd**-0.5 * LOG2E)
    me = lax.axis_index("tp")
    x, core = me // 2, me % 2
    shards = [2 * x + 1 - core, 2 * (1 - x) + 1 - core, 2 * (1 - x) + core, me]

    tiles_copy = pltpu.make_async_copy(tiles_hbm, tiles_ref, sems.at[3, 0])
    q_copies, k_copies, v_copies = [], [], []
    for b in range(count):
        q_copies.append(pltpu.make_async_copy(q_hbm.at[first + b], q_ref.at[b], sems.at[0, b]))
        k_copies.append(
            pltpu.make_async_copy(k_hbm.at[first + b], kx_ref.at[b, :, pl.ds(0, hd)], sems.at[1, b])
        )
        v_copies.append(
            pltpu.make_async_copy(v_hbm.at[first + b], vx_ref.at[b, :, pl.ds(0, hd)], sems.at[2, b])
        )
    hidden_copy = pltpu.make_async_copy(hidden_hbm.at[pl.ds(first, count)], hidden_ref, sems.at[3, 1])
    mine_copies = [
        pltpu.make_async_copy(mine_ref.at[b], mine_hbm[b], sems.at[6, b]) for b in range(count)
    ]
    w_copies, out_copies = [], []
    for s in range(4):
        cols = pl.ds(pl.multiple_of(shards[s] * shard_cols, 128), shard_cols)
        into = w_ref.at[s // 2, :, pl.ds(s % 2 * shard_cols, shard_cols)]
        w_copies.append(pltpu.make_async_copy(w_hbm.at[:, cols], into, sems.at[4, s]))
        if s < 3:
            out_copies.append([
                pltpu.make_async_copy(
                    part_ref.at[s, pl.ds(b * nodes, nodes)],
                    send_hbm[b].at[s] if s < 2 else keep_hbm[b],
                    sems.at[7 + s, b],
                )
                for b in range(count)
            ])
    tiles_copy.start()
    for b in range(count):
        q_copies[b].start()
    for b in range(count):
        k_copies[b].start()
        v_copies[b].start()

    tile_of = lax.broadcasted_iota(jnp.int32, (places, hd), 0) // TILE
    lane_of = lax.broadcasted_iota(jnp.int32, (places, hd), 1)
    marks = jnp.where(tile_of == lane_of, 1.0, 0.0).astype(jnp.bfloat16)
    for b in range(count):
        kx_ref[b, :, hd:] = marks
        vx_ref[b, :, hd:] = jnp.ones((places, hd), jnp.bfloat16)
    attn_ref[...] = jnp.zeros_like(attn_ref)

    sub = lax.broadcasted_iota(jnp.int32, (nodes, nodes), 0)
    lane = lax.broadcasted_iota(jnp.int32, (nodes, nodes), 1)
    sub_f, lane_f = sub.astype(jnp.float32), lane.astype(jnp.float32)
    tiles_copy.wait()
    for b in range(count):
        live = live_ref[first + b]
        tiles_row = jnp.broadcast_to(tiles_ref[first + b : first + b + 1, :], (nodes, nodes))
        reach_row = jnp.where(lane < live, tiles_row, 0)
        key_row = (reach_row * nodes + (nodes - 1 - lane)).astype(jnp.float32)
        key_col = key_row.T
        rank_row = jnp.sum(jnp.where(key_col > key_row, 1.0, 0.0), axis=0, keepdims=True)
        rank_col = jnp.sum(jnp.where(key_row > key_col, 1.0, 0.0), axis=1, keepdims=True)
        alive = (rank_col == lane_f) & (sub < live)
        perm_ref[b] = jnp.where(alive, 1.0, 0.0).astype(jnp.bfloat16)
        to_sorted = rank_row == sub_f
        reach = jnp.sum(
            jnp.where(to_sorted, reach_row.astype(jnp.float32), 0.0), axis=1, keepdims=True
        )
        for g in range(groups):
            longest = jnp.max(reach[g * GROUP : (g + 1) * GROUP]).astype(jnp.int32)
            segs_ref[b * groups + g] = (longest * TILE + SEG - 1) // SEG
        hidden_from = (lane_f >= jnp.maximum(reach, 1.0)) & (lane < places // TILE)
        bias = jnp.where(hidden_from, MASKED, 0.0)[:, :hd].astype(jnp.bfloat16)
        q_copies[b].wait()
        q_sorted = jnp.dot(
            jnp.where(to_sorted, 1.0, 0.0).astype(jnp.bfloat16), q_ref[b],
            preferred_element_type=jnp.float32,
        ).astype(jnp.bfloat16)
        for g in range(groups):
            for h in range(heads):
                at = slice((b * groups + g) * rows + h * GROUP, (b * groups + g) * rows + (h + 1) * GROUP)
                qx_ref[at, :hd] = q_sorted[g * GROUP : (g + 1) * GROUP, h * hd : (h + 1) * hd]
                qx_ref[at, hd:] = bias[g * GROUP : (g + 1) * GROUP]

    for b in range(count):
        k_copies[b].wait()
        v_copies[b].wait()
        if b == 0:
            for s in range(4):
                w_copies[s].start()
            hidden_copy.start()

        @pl.loop(0, (live_ref[first + b] + GROUP - 1) // GROUP)
        def _(g):
            at = pl.ds(pl.multiple_of((b * groups + g) * rows, GROUP), rows)
            out_at = pl.ds(pl.multiple_of(b * nodes + g * GROUP, GROUP), GROUP)
            segs = segs_ref[b * groups + g]

            def attend(n):
                mixed = group_softmax(n, qx_ref[at, :], kx_ref, vx_ref, b, scale, hd)
                for h in range(heads):
                    attn_ref[out_at, h * hd : (h + 1) * hd] = mixed[h * GROUP : (h + 1) * GROUP]

            def pick(low, high):
                if low == high:
                    attend(low)
                else:
                    half = (low + high) // 2
                    pl.when(segs <= half)(functools.partial(pick, low, half))
                    pl.when(segs > half)(functools.partial(pick, half + 1, high))

            pick(1, places // SEG)

    for b in range(count):
        at = slice(b * nodes, (b + 1) * nodes)
        attn_ref[at, :] = jnp.dot(
            perm_ref[b], attn_ref[at, :], preferred_element_type=jnp.float32
        ).astype(jnp.bfloat16)
    w_copies[0].wait()
    w_copies[1].wait()
    part = jnp.dot(attn_ref[...], w_ref[0], preferred_element_type=jnp.float32)
    for s in range(2):
        part_ref[s] = part[:, s * shard_cols : (s + 1) * shard_cols].astype(jnp.bfloat16)
        for copy in out_copies[s]:
            copy.start()
    w_copies[2].wait()
    w_copies[3].wait()
    hidden_copy.wait()
    part = jnp.dot(attn_ref[...], w_ref[1], preferred_element_type=jnp.float32)
    part_ref[2] = part[:, :shard_cols].astype(jnp.bfloat16)
    for copy in out_copies[2]:
        copy.start()
    row = lax.broadcasted_iota(jnp.int32, (nodes, shard_cols), 0)
    for b in range(count):
        own = part[b * nodes : (b + 1) * nodes, shard_cols:]
        mine_ref[b] = jnp.where(
            row < live_ref[first + b], own + hidden_ref[b].astype(jnp.float32), 0.0
        )
        mine_copies[b].start()
    for copy in out_copies[0] + out_copies[1] + out_copies[2] + mine_copies:
        copy.wait()


def block_partials(first, count, q, k, v, hidden, tiles, live, w, order):
    _, nodes, width = q.shape
    places, hd = k.shape[1], k.shape[2]
    heads = width // hd
    cols = w.shape[1] // 4
    bf16, f32 = jnp.bfloat16, jnp.float32
    outs = (
        [jax.ShapeDtypeStruct((2, nodes, cols), bf16)] * count
        + [jax.ShapeDtypeStruct((nodes, cols), bf16)] * count
        + [jax.ShapeDtypeStruct((nodes, cols), f32)] * count
    )
    anywhere = pl.BlockSpec(memory_space=pl.ANY)
    grid_spec = pltpu.PrefetchScalarGridSpec(
        num_scalar_prefetch=1,
        grid=(1,),
        in_specs=[anywhere] * 7,
        out_specs=[anywhere] * len(outs),
        scratch_shapes=[
            pltpu.VMEM(tiles.shape, jnp.int32),
            pltpu.VMEM((count, nodes, cols), jnp.bfloat16),
            pltpu.VMEM((count, nodes, cols), jnp.float32),
            pltpu.VMEM((count, nodes, width), jnp.bfloat16),
            pltpu.VMEM((2, width, 2 * cols), jnp.bfloat16),
            pltpu.VMEM((count, places, 2 * hd), jnp.bfloat16),
            pltpu.VMEM((count, places, 2 * hd), jnp.bfloat16),
            pltpu.VMEM((count * heads * nodes, 2 * hd), jnp.bfloat16),
            pltpu.VMEM((count * nodes, width), jnp.bfloat16),
            pltpu.VMEM((count, nodes, nodes), jnp.bfloat16),
            pltpu.VMEM((3, count * nodes, cols), jnp.bfloat16),
            pltpu.SMEM((count * (nodes // GROUP),), jnp.int32),
            pltpu.SemaphoreType.DMA((10, max(4, count))),
        ],
    )
    return pl.pallas_call(
        functools.partial(blocks_kernel, first, count),
        grid_spec=grid_spec,
        out_shape=outs,
        compiler_params=pltpu.CompilerParams(vmem_limit_bytes=VMEM_LIMIT),
        cost_estimate=pl.CostEstimate(
            flops=2 * count * nodes * width * (2 * places + w.shape[1]),
            bytes_accessed=w.size * 2 + count * 4 * places * hd,
            transcendentals=count * nodes * heads * places,
        ),
    )(live, q, k, v, hidden, tiles, w, order)


def on_device(
    kv_keys, kv_values, queries, hidden, out_weight, block_live, node_tiles, left_count, right_count
):
    blocks, _, _ = queries.shape
    tp = lax.axis_size("tp")
    ring = lax.axis_size("blk")
    to_mate = [(i, i ^ 1) for i in range(tp)]
    to_across = [(i, i ^ 2) for i in range(tp)]
    to_next = [(i, (i + 1) % ring) for i in range(ring)]
    to_prev = [(i, (i - 1) % ring) for i in range(ring)]
    left, right = left_count[0], right_count[0]
    from_prev, own, from_next = [None] * S_MAX, [None] * blocks, [None] * S_MAX
    bf16, wide = jnp.bfloat16, jnp.float32
    zero = jnp.zeros((), bf16)
    sums = {}
    order = node_tiles
    for first, count in CHUNKS:
        outs = block_partials(
            first, count, queries, kv_keys, kv_values, hidden, node_tiles, block_live,
            out_weight, order,
        )
        for b in range(count):
            j = first + b
            send, keep, mine = outs[b], outs[count + b], outs[2 * count + b]
            got = lax.ppermute(send, "tp", to_mate)
            across = (keep.astype(wide) + got[1].astype(wide)).astype(bf16)
            other = lax.ppermute(across, "tp", to_across)
            sums[j] = (mine, got[0], other)
            order = across
    for j in range(blocks):
        mine, mates, other = sums[j]
        result = (mine + mates.astype(wide) + other.astype(wide)).astype(bf16)
        own[j] = jnp.zeros_like(result)
        if 0 < j < blocks - 1:
            own[j] = jnp.where((left <= j) & (j < blocks - right), result, zero)
        if j < S_MAX:
            sent = result if j == 0 else jnp.where(j < left, result, zero)
            from_next[j] = lax.ppermute(sent, "blk", to_prev)
        if j >= blocks - S_MAX:
            sent = result if j == blocks - 1 else jnp.where(blocks - j <= right, result, zero)
            from_prev[j - blocks + S_MAX] = lax.ppermute(sent, "blk", to_next)
    return jnp.stack(from_prev + own + from_next)


def solution(mesh):
    return jax.shard_map(
        on_device,
        mesh=mesh,
        in_specs=(
            P("blk", None, "tp"),
            P("blk", None, "tp"),
            P("blk", None, "tp"),
            P("blk", None, "tp"),
            P("tp", None),
            P("blk"),
            P("blk", None),
            P("blk"),
            P("blk"),
        ),
        out_specs=P("blk", None, "tp"),
        check_vma=False,
    )
```

time: 219 us -> 59.1 us (0.27)
  matrix products: 62.1 us -> 0 us
  waiting for transfers between devices: 79.9 us -> 19.1 us
  other arithmetic: 48.3 us -> 2.55 us
  Pallas kernels: 0 us -> 20.4 us
  between operations: 14.8 us -> 1.48 us
  starting transfers between devices: 9.5 us -> 13.2 us
  local copies, waits for them, and re-layouts: 4.4 us -> 2.07 us
    reduce_scatter x1 -> x0, waiting for transfers between devices: 67.4 us -> none  [finish(): lax.psum_scatter(partial_value, 'tp', scatter_dimension=1, tiled=True)]
    dot_general x3 -> x0, matrix products: 62.1 us -> none  [the longest x1 40.3 us: attend(): jnp.einsum('srp,spd->srd', weights, value_rows, preferred_element_type=jn...]
    sub x1 -> x0, other arithmetic: 42.8 us -> none  [attend(): weights_exp = jnp.where(inside, jnp.exp(scores - row_max), jnp.float32(0.0))]
    pallas_call x0 -> x2, Pallas kernels: none -> 20.4 us  [block_partials(): pl.pallas_call(functools.partial(blocks_kernel, first, count), grid_spec=...]
    ppermute x4 -> x12, waiting for transfers between devices: 12.5 us -> 19.1 us  [the longest x2 9.7 us: on_device(): from_prev[j - blocks + S_MAX] = lax.ppermute(sent, 'blk', to_next)]
    ppermute x4 -> x12, starting transfers between devices: 9.5 us -> 13.2 us  [the longest x2 5.82 us: on_device(): from_next[j] = lax.ppermute(sent, 'blk', to_prev)]
    select_n x2, other arithmetic: 2.77 us -> 0.19 us  [the longest x1 0.09 us: on_device(): sent = result if j == 0 else jnp.where(j < left, result, zero)]
  transfers between devices with their start and end apart: 5 -> 12, of which waited for: 3 -> 5; matrix products, arithmetic and copies ran while one was open for 1% -> 5% of each run, Pallas kernels for 0% -> 17%
where the time goes in v2:
time: 59.1 us; the launch traced here: 58.9 us
  Pallas kernels  20.4 us (35%)
  waiting for transfers between devices  19.1 us (32%)
  starting transfers between devices  13.2 us (22%)
  other arithmetic  2.55 us (4%)
  local copies, waits for them, and re-layouts  2.07 us (4%)
  between operations  1.48 us (3%)
    pallas_call x2, Pallas kernels, block_partials(): pl.pallas_call(functools.partial(blocks_kernel, first, count), grid_spec=...  20.4 us
    ppermute x2, waiting for transfers between devices, on_device(): from_prev[j - blocks + S_MAX] = lax.ppermute(sent, 'blk', to_next)  9.7 us
    ppermute x4, waiting for transfers between devices, on_device(): other = lax.ppermute(across, 'tp', to_across)  9.17 us
    ppermute x2, starting transfers between devices, on_device(): from_next[j] = lax.ppermute(sent, 'blk', to_prev)  5.82 us
    ppermute x4, starting transfers between devices, on_device(): other = lax.ppermute(across, 'tp', to_across)  5.16 us
    convert_element_type x4, other arithmetic, on_device(): across = (keep.astype(wide) + got[1].astype(wide)).astype(bf16)  2.1 us
    unnamed x21, local copies, waits for them, and re-layouts  1.37 us
    ppermute x4, starting transfers between devices, on_device(): got = lax.ppermute(send, 'tp', to_mate)  1.2 us
  transfers between devices with their start and end apart: 12, of which 5 were waited for; matrix products, arithmetic and copies ran while one was open for 5% of the time, Pallas kernels for 17%

profile of v2, /device:TPU:0, one launch (start us, length us, event | category | flops | bytes accessed | tf_op | source)
XLA Modules:
  0.0 58.9 jit_solution(2141685413355423796)
XLA Ops:
  0.0 10.5 %shard_map.91 = (bf16[2,128,896]{2,1,0:T(8,128)(2,1)}, bf16[2,128,896]{2,1,0:T(8,128)(2,1)}, bf16[128,896]{1,0:T(8,128)(2,1)}, bf16[128,896]{1,0:T(8,128)(2,1)}, f32[128,896]{1,0:T(8,128)}, /*index=5*/f32[128,896]{1,0:T(8,128)}) custom-call(s32[4]{0:T(128)} %live_ref.3, bf16[4,128,896]{2,1,0:T(8,128)(2,1)} %q_hbm.3, bf16[4,2048,128]{2,1,0:T(8,128)(2,1)} %k_hbm.3, ...), custom_call_target="tpu_custom_call" | custom-call | flops 3523215360 | bytes 8519680 | tf_op jit(solution)/shard_map/pallas_call | solution.py:228
  10.5 0.6 collective-permute-start
  11.1 0.1 collective-permute-start.8
  12.4 0.3 collective-permute-done
  12.7 1.0 %fusion.11.order_hbm = bf16[128,896]{1,0:T(8,128)(2,1)S(1)} fusion(bf16[128,896]{1,0:T(8,128)(2,1)} %get-tuple-element.17, bf16[2,128,896]{2,1,0:T(8,128)(2,1)S(1)} %collective-permute-done), kind=kLoop, calls=%fused_computation.19 | loop fusion | flops 458752 | bytes 688128 | tf_op jit(solution)/shard_map/convert_element_type | solution.py:266
  13.7 0.0 copy-start.6
  13.7 2.9 %collective-permute-start.7 = (bf16[128,896]{1,0:T(8,128)(2,1)S(1)}, bf16[128,896]{1,0:T(8,128)(2,1)S(1)}, u32[]{:S(2)}, u32[]{:S(2)}) collective-permute-start(bf16[128,896]{1,0:T(8,128)(2,1)S(1)} %fusion.11.order_hbm), channel_id=1, source_target_pairs={{0,2},{1,3},{2,0},{3,1},{4,6},{5,7},{6,4},{7,5},{8,10},{9,11},{10,... | collective-permute-start | bytes 688136 | tf_op jit(solution)/shard_map/ppermute | solution.py:267
  16.6 0.0 collective-permute-done.8
  16.6 1.0 %fusion = bf16[128,896]{1,0:T(8,128)(2,1)S(1)} fusion(bf16[128,896]{1,0:T(8,128)(2,1)} %get-tuple-element.28, bf16[2,128,896]{2,1,0:T(8,128)(2,1)S(1)} %collective-permute-done.8), kind=kLoop, calls=%fused_computation.1 | loop fusion | flops 458752 | bytes 688128 | tf_op jit(solution)/shard_map/convert_element_type | solution.py:266
  17.6 0.0 copy-start.2
  17.6 0.0 copy-start
  17.7 0.1 collective-permute-start.9
  17.7 0.0 copy-done.6
  17.8 9.9 %shard_map.92 = (bf16[2,128,896]{2,1,0:T(8,128)(2,1)}, bf16[2,128,896]{2,1,0:T(8,128)(2,1)}, bf16[128,896]{1,0:T(8,128)(2,1)}, bf16[128,896]{1,0:T(8,128)(2,1)}, f32[128,896]{1,0:T(8,128)}, /*index=5*/f32[128,896]{1,0:T(8,128)}) custom-call(s32[4]{0:T(128)} %live_ref.3, bf16[4,128,896]{2,1,0:T(8,128)(2,1)} %q_hbm.3, bf16[4,2048,128]{2,1,0:T(8,128)(2,1)} %k_hbm.3, ...), custom_call_target="tpu_custom_call" | custom-call | flops 3523215360 | bytes 8519680 | tf_op jit(solution)/shard_map/pallas_call | solution.py:228
  27.7 0.0 copy-start.5
  27.7 0.0 copy-start.4
  27.7 0.1 collective-permute-start.1
  27.8 0.5 collective-permute-start.4
  28.3 0.0 collective-permute-done.7
  28.3 0.0 copy-done.2
  28.3 0.1 broadcast_select_fusion
  28.4 4.2 %collective-permute-start.11 = (bf16[128,896]{1,0:T(8,128)(2,1)S(1)}, bf16[128,896]{1,0:T(8,128)(2,1)S(1)}, u32[]{:S(2)}, u32[]{:S(2)}) collective-permute-start(bf16[128,896]{1,0:T(8,128)(2,1)S(1)} %get-tuple-element.29), channel_id=1, source_target_pairs={{0,28},{4,0},{8,4},{12,8},{16,12},{20,16},{24,20},{28,24},{1,29},{... | collective-permute-start | bytes 688136 | tf_op jit(solution)/shard_map/ppermute | solution.py:278
  32.6 0.0 collective-permute-done.9
  32.6 0.0 copy-done
  32.6 0.1 fusion.2
  32.7 1.6 %collective-permute-start.10 = (bf16[128,896]{1,0:T(8,128)(2,1)S(1)}, bf16[128,896]{1,0:T(8,128)(2,1)S(1)}, u32[]{:S(2)}, u32[]{:S(2)}) collective-permute-start(bf16[128,896]{1,0:T(8,128)(2,1)S(1)} %fusion.2), channel_id=1, source_target_pairs={{0,28},{4,0},{8,4},{12,8},{16,12},{20,16},{24,20},{28,24},{1,29},{... | collective-permute-start | bytes 688136 | tf_op jit(solution)/shard_map/ppermute | solution.py:278
  34.3 0.0 collective-permute-done.1
  34.3 0.0 copy-done.5
  34.3 0.1 fusion.8
  34.4 1.6 %collective-permute-start.2 = (bf16[128,896]{1,0:T(8,128)(2,1)S(1)}, bf16[128,896]{1,0:T(8,128)(2,1)S(1)}, u32[]{:S(2)}, u32[]{:S(2)}) collective-permute-start(bf16[128,896]{1,0:T(8,128)(2,1)S(1)} %fusion.8), channel_id=1, source_target_pairs={{0,2},{1,3},{2,0},{3,1},{4,6},{5,7},{6,4},{7,5},{8,10},{9,11},{10,... | collective-permute-start | bytes 688136 | tf_op jit(solution)/shard_map/ppermute | solution.py:267
  35.9 0.0 collective-permute-done.4
  35.9 0.1 fusion.5
  36.0 0.6 %collective-permute-start.5 = (bf16[128,896]{1,0:T(8,128)(2,1)S(1)}, bf16[128,896]{1,0:T(8,128)(2,1)S(1)}, u32[]{:S(2)}, u32[]{:S(2)}) collective-permute-start(bf16[128,896]{1,0:T(8,128)(2,1)S(1)} %fusion.5), channel_id=1, source_target_pairs={{0,2},{1,3},{2,0},{3,1},{4,6},{5,7},{6,4},{7,5},{8,10},{9,11},{10,... | collective-permute-start | bytes 688136 | tf_op jit(solution)/shard_map/ppermute | solution.py:267
  36.6 6.3 %collective-permute-done.2 = bf16[128,896]{1,0:T(8,128)(2,1)S(1)} collective-permute-done((bf16[128,896]{1,0:T(8,128)(2,1)S(1)}, bf16[128,896]{1,0:T(8,128)(2,1)S(1)}, u32[]{:S(2)}, u32[]{:S(2)}) %collective-permute-start.2) | collective-permute-done | bytes 229408 | tf_op jit(solution)/shard_map/ppermute | solution.py:267
  42.9 0.1 broadcast_select_fusion.1
  43.0 0.5 collective-permute-start.3
  43.5 2.8 %collective-permute-done.5 = bf16[128,896]{1,0:T(8,128)(2,1)S(1)} collective-permute-done((bf16[128,896]{1,0:T(8,128)(2,1)S(1)}, bf16[128,896]{1,0:T(8,128)(2,1)S(1)}, u32[]{:S(2)}, u32[]{:S(2)}) %collective-permute-start.5) | collective-permute-done | bytes 229408 | tf_op jit(solution)/shard_map/ppermute | solution.py:267
  46.4 0.1 fusion.7
  46.4 0.5 collective-permute-start.6
  47.0 6.1 %collective-permute-done.3 = bf16[128,896]{1,0:T(8,128)(2,1)S(1)} collective-permute-done((bf16[128,896]{1,0:T(8,128)(2,1)S(1)}, bf16[128,896]{1,0:T(8,128)(2,1)S(1)}, u32[]{:S(2)}, u32[]{:S(2)}) %collective-permute-start.3) | collective-permute-done | bytes 229408 | tf_op jit(solution)/shard_map/ppermute | solution.py:281
  53.1 3.6 %collective-permute-done.6 = bf16[128,896]{1,0:T(8,128)(2,1)S(1)} collective-permute-done((bf16[128,896]{1,0:T(8,128)(2,1)S(1)}, bf16[128,896]{1,0:T(8,128)(2,1)S(1)}, u32[]{:S(2)}, u32[]{:S(2)}) %collective-permute-start.6) | collective-permute-done | bytes 229408 | tf_op jit(solution)/shard_map/ppermute | solution.py:281
  56.7 0.1 bitcast_dynamic-update-slice_fusion.3
  56.8 0.1 bitcast_dynamic-update-slice_fusion.2
  56.9 0.0 collective-permute-done.10
  56.9 0.0 copy-start.7
  56.9 0.0 collective-permute-done.11
  57.0 1.2 %copy-done.7 = bf16[8,128,896]{2,1,0:T(8,128)(2,1)} copy-done((bf16[8,128,896]{2,1,0:T(8,128)(2,1)}, bf16[8,128,896]{2,1,0:T(8,128)(2,1)S(1)}, u32[]{:S(2)}) %copy-start.7) | copy-done | bytes 1835032
  58.2 0.7 %bitcast_dynamic-update-slice_fusion = bf16[8,128,896]{2,1,0:T(8,128)(2,1)} fusion(bf16[8,128,896]{2,1,0:T(8,128)(2,1)} %copy-done.7, bf16[128,896]{1,0:T(8,128)(2,1)S(1)} %collective-permute-done.11), kind=kLoop, calls=%fused_computation.28 | loop fusion | bytes 458752 | tf_op jit(solution)/shard_map/stack | solution.py:282
  (10 shorter events, 0.1 us)
Async XLA Ops:
  10.5 2.2 %collective-permute-start = (bf16[2,128,896]{2,1,0:T(8,128)(2,1)}, bf16[2,128,896]{2,1,0:T(8,128)(2,1)S(1)}, u32[]{:S(2)}, u32[]{:S(2)}) collective-permute-start(bf16[2,128,896]{2,1,0:T(8,128)(2,1)} %get-tuple-element.18), channel_id=1, source_target_pairs={{0,1},{1,0},{2,3},{3,2},{4,5},{5,4},{6,7},{7,6},{8,9},{9,8},{10,11... | collective-permute-start | bytes 1376264 | tf_op jit(solution)/shard_map/ppermute | solution.py:265
  11.1 5.6 %collective-permute-start.8 = (bf16[2,128,896]{2,1,0:T(8,128)(2,1)}, bf16[2,128,896]{2,1,0:T(8,128)(2,1)S(1)}, u32[]{:S(2)}, u32[]{:S(2)}) collective-permute-start(bf16[2,128,896]{2,1,0:T(8,128)(2,1)} %get-tuple-element.27), channel_id=1, source_target_pairs={{0,1},{1,0},{2,3},{3,2},{4,5},{5,4},{6,7},{7,6},{8,9},{9,8},{10,11... | collective-permute-start | bytes 1376264 | tf_op jit(solution)/shard_map/ppermute | solution.py:265
  13.7 4.0 %copy-start.6 = (bf16[128,896]{1,0:T(8,128)(2,1)}, bf16[128,896]{1,0:T(8,128)(2,1)S(1)}, u32[]{:S(2)}) copy-start(bf16[128,896]{1,0:T(8,128)(2,1)S(1)} %fusion.11.order_hbm) | copy-start | bytes 688132
  13.7 14.6 %collective-permute-start.7 = (bf16[128,896]{1,0:T(8,128)(2,1)S(1)}, bf16[128,896]{1,0:T(8,128)(2,1)S(1)}, u32[]{:S(2)}, u32[]{:S(2)}) collective-permute-start(bf16[128,896]{1,0:T(8,128)(2,1)S(1)} %fusion.11.order_hbm), channel_id=1, source_target_pairs={{0,2},{1,3},{2,0},{3,1},{4,6},{5,7},{6,4},{7,5},{8,10},{9,11},{10,... | collective-permute-start | bytes 688136 | tf_op jit(solution)/shard_map/ppermute | solution.py:267
  17.6 10.6 %copy-start.2 = (f32[128,896]{1,0:T(8,128)S(1)}, f32[128,896]{1,0:T(8,128)}, u32[]{:S(2)}) copy-start(f32[128,896]{1,0:T(8,128)} %get-tuple-element.25) | copy-start | bytes 1376260
  17.6 14.9 %copy-start = (f32[128,896]{1,0:T(8,128)S(1)}, f32[128,896]{1,0:T(8,128)}, u32[]{:S(2)}) copy-start(f32[128,896]{1,0:T(8,128)} %get-tuple-element.26) | copy-start | bytes 1376260
  17.7 14.9 %collective-permute-start.9 = (bf16[128,896]{1,0:T(8,128)(2,1)S(1)}, bf16[128,896]{1,0:T(8,128)(2,1)S(1)}, u32[]{:S(2)}, u32[]{:S(2)}) collective-permute-start(bf16[128,896]{1,0:T(8,128)(2,1)S(1)} %fusion), channel_id=1, source_target_pairs={{0,2},{1,3},{2,0},{3,1},{4,6},{5,7},{6,4},{7,5},{8,10},{9,11},{10,... | collective-permute-start | bytes 688136 | tf_op jit(solution)/shard_map/ppermute | solution.py:267
  27.7 6.6 %copy-start.5 = (bf16[128,896]{1,0:T(8,128)(2,1)S(1)}, bf16[128,896]{1,0:T(8,128)(2,1)}, u32[]{:S(2)}) copy-start(bf16[128,896]{1,0:T(8,128)(2,1)} %get-tuple-element.21) | copy-start | bytes 688132
  27.7 8.2 %copy-start.4 = (bf16[128,896]{1,0:T(8,128)(2,1)S(1)}, bf16[128,896]{1,0:T(8,128)(2,1)}, u32[]{:S(2)}) copy-start(bf16[128,896]{1,0:T(8,128)(2,1)} %get-tuple-element.24) | copy-start | bytes 688132
  27.7 6.6 %collective-permute-start.1 = (bf16[2,128,896]{2,1,0:T(8,128)(2,1)}, bf16[2,128,896]{2,1,0:T(8,128)(2,1)S(1)}, u32[]{:S(2)}, u32[]{:S(2)}) collective-permute-start(bf16[2,128,896]{2,1,0:T(8,128)(2,1)} %get-tuple-element.20), channel_id=1, source_target_pairs={{0,1},{1,0},{2,3},{3,2},{4,5},{5,4},{6,7},{7,6},{8,9},{9,8},{10,11... | collective-permute-start | bytes 1376264 | tf_op jit(solution)/shard_map/ppermute | solution.py:265
  27.8 8.1 %collective-permute-start.4 = (bf16[2,128,896]{2,1,0:T(8,128)(2,1)}, bf16[2,128,896]{2,1,0:T(8,128)(2,1)S(1)}, u32[]{:S(2)}, u32[]{:S(2)}) collective-permute-start(bf16[2,128,896]{2,1,0:T(8,128)(2,1)} %get-tuple-element.23), channel_id=1, source_target_pairs={{0,1},{1,0},{2,3},{3,2},{4,5},{5,4},{6,7},{7,6},{8,9},{9,8},{10,11... | collective-permute-start | bytes 1376264 | tf_op jit(solution)/shard_map/ppermute | solution.py:265
  28.3 14.6 %copy-start.3 = (f32[128,896]{1,0:T(8,128)S(1)}, f32[128,896]{1,0:T(8,128)}, u32[]{:S(2)}) copy-start(f32[128,896]{1,0:T(8,128)} %get-tuple-element.19) | copy-start | bytes 1376260
  28.4 28.6 %collective-permute-start.11 = (bf16[128,896]{1,0:T(8,128)(2,1)S(1)}, bf16[128,896]{1,0:T(8,128)(2,1)S(1)}, u32[]{:S(2)}, u32[]{:S(2)}) collective-permute-start(bf16[128,896]{1,0:T(8,128)(2,1)S(1)} %get-tuple-element.29), channel_id=1, source_target_pairs={{0,28},{4,0},{8,4},{12,8},{16,12},{20,16},{24,20},{28,24},{1,29},{... | collective-permute-start | bytes 688136 | tf_op jit(solution)/shard_map/ppermute | solution.py:278
  32.6 13.8 %copy-start.1 = (f32[128,896]{1,0:T(8,128)S(1)}, f32[128,896]{1,0:T(8,128)}, u32[]{:S(2)}) copy-start(f32[128,896]{1,0:T(8,128)} %get-tuple-element.22) | copy-start | bytes 1376260
  32.7 24.2 %collective-permute-start.10 = (bf16[128,896]{1,0:T(8,128)(2,1)S(1)}, bf16[128,896]{1,0:T(8,128)(2,1)S(1)}, u32[]{:S(2)}, u32[]{:S(2)}) collective-permute-start(bf16[128,896]{1,0:T(8,128)(2,1)S(1)} %fusion.2), channel_id=1, source_target_pairs={{0,28},{4,0},{8,4},{12,8},{16,12},{20,16},{24,20},{28,24},{1,29},{... | collective-permute-start | bytes 688136 | tf_op jit(solution)/shard_map/ppermute | solution.py:278
  34.4 8.5 %collective-permute-start.2 = (bf16[128,896]{1,0:T(8,128)(2,1)S(1)}, bf16[128,896]{1,0:T(8,128)(2,1)S(1)}, u32[]{:S(2)}, u32[]{:S(2)}) collective-permute-start(bf16[128,896]{1,0:T(8,128)(2,1)S(1)} %fusion.8), channel_id=1, source_target_pairs={{0,2},{1,3},{2,0},{3,1},{4,6},{5,7},{6,4},{7,5},{8,10},{9,11},{10,... | collective-permute-start | bytes 688136 | tf_op jit(solution)/shard_map/ppermute | solution.py:267
  36.0 10.4 %collective-permute-start.5 = (bf16[128,896]{1,0:T(8,128)(2,1)S(1)}, bf16[128,896]{1,0:T(8,128)(2,1)S(1)}, u32[]{:S(2)}, u32[]{:S(2)}) collective-permute-start(bf16[128,896]{1,0:T(8,128)(2,1)S(1)} %fusion.5), channel_id=1, source_target_pairs={{0,2},{1,3},{2,0},{3,1},{4,6},{5,7},{6,4},{7,5},{8,10},{9,11},{10,... | collective-permute-start | bytes 688136 | tf_op jit(solution)/shard_map/ppermute | solution.py:267
  43.0 10.1 %collective-permute-start.3 = (bf16[128,896]{1,0:T(8,128)(2,1)S(1)}, bf16[128,896]{1,0:T(8,128)(2,1)S(1)}, u32[]{:S(2)}, u32[]{:S(2)}) collective-permute-start(bf16[128,896]{1,0:T(8,128)(2,1)S(1)} %get-tuple-element.31), channel_id=1, source_target_pairs={{0,4},{4,8},{8,12},{12,16},{16,20},{20,24},{24,28},{28,0},{1,5},{5... | collective-permute-start | bytes 688136 | tf_op jit(solution)/shard_map/ppermute | solution.py:281
  46.4 10.2 %collective-permute-start.6 = (bf16[128,896]{1,0:T(8,128)(2,1)S(1)}, bf16[128,896]{1,0:T(8,128)(2,1)S(1)}, u32[]{:S(2)}, u32[]{:S(2)}) collective-permute-start(bf16[128,896]{1,0:T(8,128)(2,1)S(1)} %fusion.7), channel_id=1, source_target_pairs={{0,4},{4,8},{8,12},{12,16},{16,20},{20,24},{24,28},{28,0},{1,5},{5... | collective-permute-start | bytes 688136 | tf_op jit(solution)/shard_map/ppermute | solution.py:281
  56.9 1.2 %copy-start.7 = (bf16[8,128,896]{2,1,0:T(8,128)(2,1)}, bf16[8,128,896]{2,1,0:T(8,128)(2,1)S(1)}, u32[]{:S(2)}) copy-start(bf16[8,128,896]{2,1,0:T(8,128)(2,1)S(1)} %bitcast_dynamic-update-slice_fusion.1) | copy-start | bytes 5505028

commit v3 on v2

v3 whole, which is shorter than its diff:
```python
import functools

import jax
import jax.numpy as jnp
from jax import lax
from jax.experimental import pallas as pl
from jax.experimental.pallas import tpu as pltpu
from jax.sharding import PartitionSpec as P


TILE = 128
S_MAX = 2
GROUP = 64
SEG = 512
LOG2E = 1.4426950408889634
MASKED = -1e30
VMEM_LIMIT = 58 << 20


def group_softmax(n, qg, kx_ref, vx_ref, b, scale, hd):
    tops, outs = [], []
    for i in range(n):
        at = slice(i * SEG, (i + 1) * SEG)
        s = lax.dot_general(
            qg, kx_ref[b, at, :], (((1,), (1,)), ((), ())), preferred_element_type=jnp.float32
        )
        top = jnp.max(s, axis=1, keepdims=True)
        p = jnp.exp2((s - top) * scale).astype(jnp.bfloat16)
        tops.append(top)
        outs.append(jnp.dot(p, vx_ref[b, at, :], preferred_element_type=jnp.float32))
    if n == 1:
        acc = outs[0]
    else:
        top = functools.reduce(jnp.maximum, tops)
        acc = sum(o * jnp.exp2((t - top) * scale) for o, t in zip(outs, tops))
    return (acc[:, :hd] / acc[:, hd:]).astype(jnp.bfloat16)


def shard_order():
    me = lax.axis_index("tp")
    x, core = me // 2, me % 2
    return [2 * x + 1 - core, 2 * (1 - x) + 1 - core, 2 * (1 - x) + core, me]


def weight_copies(w_hbm, w_ref, sems):
    cols = w_ref.shape[2] // 2
    copies = []
    for s, shard in enumerate(shard_order()):
        src = w_hbm.at[:, pl.ds(pl.multiple_of(shard * cols, 128), cols)]
        into = w_ref.at[s // 2, :, pl.ds(s % 2 * cols, cols)]
        copies.append(pltpu.make_async_copy(src, into, sems.at[s]))
    return copies


def project(attn, residual, w_ref, w_copies, part_ref, mine_ref, outs, sems):
    count, cols = len(outs) // 3, mine_ref.shape[1]
    nodes = attn.shape[0] // count
    copies = [[] for _ in range(4)]
    for b in range(count):
        at = pl.ds(b * nodes, nodes)
        to = [outs[b].at[0], outs[b].at[1], outs[count + b]]
        for s in range(3):
            copies[s].append(pltpu.make_async_copy(part_ref.at[s, at], to[s], sems.at[b, s]))
        copies[3].append(pltpu.make_async_copy(mine_ref.at[at], outs[2 * count + b], sems.at[b, 3]))
    w_copies[0].wait()
    w_copies[1].wait()
    part = jnp.dot(attn, w_ref[0], preferred_element_type=jnp.float32)
    for s in range(2):
        part_ref[s] = part[:, s * cols : (s + 1) * cols].astype(jnp.bfloat16)
        for copy in copies[s]:
            copy.start()
    w_copies[2].wait()
    w_copies[3].wait()
    part = jnp.dot(attn, w_ref[1], preferred_element_type=jnp.float32)
    part_ref[2] = part[:, :cols].astype(jnp.bfloat16)
    mine_ref[...] = part[:, cols:] + residual().astype(jnp.float32)
    for copy in copies[2] + copies[3]:
        copy.start()
    return sum(copies, [])


def attend_kernel(
    ids, shipped, live_ref, q_hbm, k_hbm, v_hbm, hidden_hbm, tiles_hbm, w_hbm, *refs,
):
    made = len(ids) - shipped
    outs, refs = refs[: 3 * made + shipped], refs[3 * made + shipped :]
    (
        tiles_ref, hidden_ref, ship_ref, q_ref, w_ref, kx_ref, vx_ref, qx_ref, attn_ref, perm_ref,
        part_ref, mine_ref, segs_ref, sems, out_sems,
    ) = refs
    count, nodes, width = q_ref.shape
    places, hd = kx_ref.shape[1], kx_ref.shape[2] // 2
    heads = width // hd
    groups = nodes // GROUP
    rows = heads * GROUP
    scale = jnp.float32(hd**-0.5 * LOG2E)

    tiles_copy = pltpu.make_async_copy(tiles_hbm, tiles_ref, sems.at[3, 0])
    q_copies, k_copies, v_copies, hidden_copies = [], [], [], []
    for b, j in enumerate(ids):
        q_copies.append(pltpu.make_async_copy(q_hbm.at[j], q_ref.at[b], sems.at[0, b]))
        k_copies.append(
            pltpu.make_async_copy(k_hbm.at[j], kx_ref.at[b, :, pl.ds(0, hd)], sems.at[1, b])
        )
        v_copies.append(
            pltpu.make_async_copy(v_hbm.at[j], vx_ref.at[b, :, pl.ds(0, hd)], sems.at[2, b])
        )
        into = hidden_ref.at[pl.ds(b * nodes, nodes)]
        hidden_copies.append(pltpu.make_async_copy(hidden_hbm.at[j], into, sems.at[6, b]))
    w_copies = weight_copies(w_hbm, w_ref, sems.at[4])
    tiles_copy.start()
    for b in range(count):
        q_copies[b].start()
    for b in range(count):
        k_copies[b].start()
        v_copies[b].start()

    tile_of = lax.broadcasted_iota(jnp.int32, (places, hd), 0) // TILE
    lane_of = lax.broadcasted_iota(jnp.int32, (places, hd), 1)
    marks = jnp.where(tile_of == lane_of, 1.0, 0.0).astype(jnp.bfloat16)
    for b in range(count):
        kx_ref[b, :, hd:] = marks
        vx_ref[b, :, hd:] = jnp.ones((places, hd), jnp.bfloat16)
    attn_ref[...] = jnp.zeros_like(attn_ref)

    sub = lax.broadcasted_iota(jnp.int32, (nodes, nodes), 0)
    lane = lax.broadcasted_iota(jnp.int32, (nodes, nodes), 1)
    sub_f, lane_f = sub.astype(jnp.float32), lane.astype(jnp.float32)
    tiles_copy.wait()
    for b, j in enumerate(ids):
        live = live_ref[j]
        tiles_row = jnp.broadcast_to(tiles_ref[j : j + 1, :], (nodes, nodes))
        reach_row = jnp.where(lane < live, tiles_row, 0)
        key_row = (reach_row * nodes + (nodes - 1 - lane)).astype(jnp.float32)
        key_col = key_row.T
        rank_row = jnp.sum(jnp.where(key_col > key_row, 1.0, 0.0), axis=0, keepdims=True)
        rank_col = jnp.sum(jnp.where(key_row > key_col, 1.0, 0.0), axis=1, keepdims=True)
        alive = (rank_col == lane_f) & (sub < live)
        perm_ref[b] = jnp.where(alive, 1.0, 0.0).astype(jnp.bfloat16)
        to_sorted = rank_row == sub_f
        reach = jnp.sum(
            jnp.where(to_sorted, reach_row.astype(jnp.float32), 0.0), axis=1, keepdims=True
        )
        for g in range(groups):
            longest = jnp.max(reach[g * GROUP : (g + 1) * GROUP]).astype(jnp.int32)
            segs_ref[b * groups + g] = (longest * TILE + SEG - 1) // SEG
        hidden_from = (lane_f >= jnp.maximum(reach, 1.0)) & (lane < places // TILE)
        bias = jnp.where(hidden_from, MASKED, 0.0)[:, :hd].astype(jnp.bfloat16)
        q_copies[b].wait()
        q_sorted = jnp.dot(
            jnp.where(to_sorted, 1.0, 0.0).astype(jnp.bfloat16), q_ref[b],
            preferred_element_type=jnp.float32,
        ).astype(jnp.bfloat16)
        for g in range(groups):
            for h in range(heads):
                start = (b * groups + g) * rows + h * GROUP
                at = slice(start, start + GROUP)
                qx_ref[at, :hd] = q_sorted[g * GROUP : (g + 1) * GROUP, h * hd : (h + 1) * hd]
                qx_ref[at, hd:] = bias[g * GROUP : (g + 1) * GROUP]

    def alive_residual(b):
        row = lax.broadcasted_iota(jnp.int32, (nodes, hidden_ref.shape[1]), 0)
        residual = hidden_ref[b * nodes : (b + 1) * nodes, :]
        return jnp.where(row < live_ref[ids[b]], residual, jnp.zeros((), residual.dtype))

    ship_copies = []
    for b, j in enumerate(ids):
        k_copies[b].wait()
        v_copies[b].wait()
        if b == 0:
            for copy in hidden_copies + w_copies:
                copy.start()

        @pl.loop(0, (live_ref[j] + GROUP - 1) // GROUP)
        def _(g):
            at = pl.ds(pl.multiple_of((b * groups + g) * rows, GROUP), rows)
            out_at = pl.ds(pl.multiple_of(b * nodes + g * GROUP, GROUP), GROUP)
            segs = segs_ref[b * groups + g]

            def attend(n):
                mixed = group_softmax(n, qx_ref[at, :], kx_ref, vx_ref, b, scale, hd)
                for h in range(heads):
                    attn_ref[out_at, h * hd : (h + 1) * hd] = mixed[h * GROUP : (h + 1) * GROUP]

            def pick(low, high):
                if low == high:
                    attend(low)
                else:
                    half = (low + high) // 2
                    pl.when(segs <= half)(functools.partial(pick, low, half))
                    pl.when(segs > half)(functools.partial(pick, half + 1, high))

            pick(1, places // SEG)

        at = slice(b * nodes, (b + 1) * nodes)
        in_place = jnp.dot(
            perm_ref[b], attn_ref[at, :], preferred_element_type=jnp.float32
        ).astype(jnp.bfloat16)
        if b < shipped:
            ship_ref[0] = in_place
            hidden_copies[b].wait()
            ship_ref[1] = alive_residual(b)
            ship_copies.append(pltpu.make_async_copy(ship_ref, outs[3 * made], sems.at[3, 1]))
            ship_copies[0].start()
        else:
            attn_ref[at, :] = in_place

    def residual():
        for copy in hidden_copies[shipped:]:
            copy.wait()
        return jnp.concatenate([alive_residual(b) for b in range(shipped, count)], axis=0)

    out_copies = project(
        attn_ref[shipped * nodes :, :], residual, w_ref, w_copies, part_ref, mine_ref,
        outs[: 3 * made], out_sems,
    )
    for copy in ship_copies + out_copies:
        copy.wait()


def project_kernel(
    moved_hbm, w_hbm, send_hbm, keep_hbm, mine_hbm, moved_ref, w_ref, part_ref, mine_ref, sems,
    out_sems,
):
    moved_copy = pltpu.make_async_copy(moved_hbm, moved_ref, sems.at[2, 0])
    moved_copy.start()
    w_copies = weight_copies(w_hbm, w_ref, sems.at[0])
    for copy in w_copies:
        copy.start()
    moved_copy.wait()
    out_copies = project(
        moved_ref[0], lambda: moved_ref[1], w_ref, w_copies, part_ref, mine_ref,
        (send_hbm, keep_hbm, mine_hbm), out_sems,
    )
    for copy in out_copies:
        copy.wait()


def partial_shapes(count, rows, cols):
    return (
        [pltpu.VMEM((2, rows, cols), jnp.bfloat16)] * count
        + [pltpu.VMEM((rows, cols), jnp.bfloat16)] * count
        + [pltpu.VMEM((rows, cols), jnp.float32)] * count
    )


def attend_blocks(ids, shipped, q, k, v, hidden, tiles, live, w):
    _, nodes, width = q.shape
    places, hd = k.shape[1], k.shape[2]
    heads = width // hd
    cols = hidden.shape[2]
    count = len(ids)
    made = (count - shipped) * nodes
    bf16 = jnp.bfloat16
    outs = partial_shapes(count - shipped, nodes, cols)
    outs += [jax.ShapeDtypeStruct((2, nodes, cols), bf16)] * shipped
    anywhere = pl.BlockSpec(memory_space=pl.ANY)
    grid_spec = pltpu.PrefetchScalarGridSpec(
        num_scalar_prefetch=1,
        grid=(1,),
        in_specs=[anywhere] * 6,
        out_specs=[anywhere] * len(outs),
        scratch_shapes=[
            pltpu.VMEM(tiles.shape, jnp.int32),
            pltpu.VMEM((count * nodes, cols), bf16),
            pltpu.VMEM((2, nodes, cols), bf16),
            pltpu.VMEM((count, nodes, width), bf16),
            pltpu.VMEM((2, width, 2 * cols), bf16),
            pltpu.VMEM((count, places, 2 * hd), bf16),
            pltpu.VMEM((count, places, 2 * hd), bf16),
            pltpu.VMEM((count * heads * nodes, 2 * hd), bf16),
            pltpu.VMEM((count * nodes, width), bf16),
            pltpu.VMEM((count, nodes, nodes), bf16),
            pltpu.VMEM((3, made, cols), bf16),
            pltpu.VMEM((made, cols), jnp.float32),
            pltpu.SMEM((count * (nodes // GROUP),), jnp.int32),
            pltpu.SemaphoreType.DMA((7, max(4, count))),
            pltpu.SemaphoreType.DMA((count - shipped, 4)),
        ],
    )
    return pl.pallas_call(
        functools.partial(attend_kernel, ids, shipped),
        grid_spec=grid_spec,
        out_shape=outs,
        compiler_params=pltpu.CompilerParams(vmem_limit_bytes=VMEM_LIMIT),
        cost_estimate=pl.CostEstimate(
            flops=4 * count * nodes * width * places + 2 * made * width * w.shape[1],
            bytes_accessed=w.size * 2 + count * 4 * places * hd,
            transcendentals=count * nodes * heads * places,
        ),
    )(live, q, k, v, hidden, tiles, w)


def project_block(moved, w):
    _, nodes, cols = moved.shape
    width = w.shape[0]
    outs = partial_shapes(1, nodes, cols)
    anywhere = pl.BlockSpec(memory_space=pl.ANY)
    return pl.pallas_call(
        project_kernel,
        in_specs=[anywhere] * 2,
        out_specs=[anywhere] * len(outs),
        scratch_shapes=[
            pltpu.VMEM(moved.shape, jnp.bfloat16),
            pltpu.VMEM((2, width, 2 * cols), jnp.bfloat16),
            pltpu.VMEM((3, nodes, cols), jnp.bfloat16),
            pltpu.VMEM((nodes, cols), jnp.float32),
            pltpu.SemaphoreType.DMA((3, 4)),
            pltpu.SemaphoreType.DMA((1, 4)),
        ],
        out_shape=outs,
        compiler_params=pltpu.CompilerParams(vmem_limit_bytes=VMEM_LIMIT),
        cost_estimate=pl.CostEstimate(
            flops=2 * nodes * width * w.shape[1], bytes_accessed=w.size * 2, transcendentals=0
        ),
    )(moved, w)


def on_device(
    kv_keys, kv_values, queries, hidden, out_weight, block_live, node_tiles, left_count, right_count
):
    blocks, nodes, _ = queries.shape
    tp = lax.axis_size("tp")
    ring = lax.axis_size("blk")
    to_mate = [(i, i ^ 1) for i in range(tp)]
    to_across = [(i, i ^ 2) for i in range(tp)]
    to_next = [(i, (i + 1) % ring) for i in range(ring)]
    to_prev = [(i, (i - 1) % ring) for i in range(ring)]
    bf16, wide = jnp.bfloat16, jnp.float32

    left, right = left_count[0], right_count[0]
    zero = jnp.zeros((), jnp.bfloat16)

    def attend(ids, shipped):
        return attend_blocks(
            ids, shipped, queries, kv_keys, kv_values, hidden, node_tiles, block_live,
            out_weight,
        )

    def sum_start(send, keep):
        got = lax.ppermute(send, "tp", to_mate)
        across = (keep.astype(wide) + got[1].astype(wide)).astype(bf16)
        return got[0], lax.ppermute(across, "tp", to_across)

    def total(mine, mates, other):
        return mine + mates.astype(wide) + other.astype(wide)

    last = blocks - 1
    out = jnp.zeros((blocks + 2 * S_MAX, nodes, hidden.shape[2]), bf16)
    send0, send1, keep0, keep1, mine0, mine1, ship = attend((last, 0, 1), 1)
    moved = lax.ppermute(ship, "blk", to_next)
    mates0, other0 = sum_start(send0, keep0)
    mates1, other1 = sum_start(send1, keep1)
    send2, keep2, mine2 = attend((2,), 0)
    mates2, other2 = sum_start(send2, keep2)
    send3, keep3, mine3 = project_block(moved, out_weight)
    mates3, other3 = sum_start(send3, keep3)

    def masked(value, kept):
        return jnp.where(kept, value.astype(bf16), zero)

    from_next0 = lax.ppermute(total(mine0, mates0, other0).astype(bf16), "blk", to_prev)
    result = total(mine1, mates1, other1)
    own1 = masked(result, (left <= 1) & (1 < blocks - right))
    from_next1 = lax.ppermute(masked(result, 1 < left), "blk", to_prev)
    result = total(mine2, mates2, other2)
    own2 = masked(result, (left <= 2) & (2 < blocks - right))
    from_prev = lax.ppermute(masked(result, blocks - 2 <= right), "blk", to_next)
    out = out.at[S_MAX + 1].set(own1)
    out = out.at[S_MAX + 2].set(own2)
    out = out.at[S_MAX + blocks].set(from_next0)
    out = out.at[S_MAX + blocks + 1].set(from_next1)
    out = out.at[1].set(total(mine3, mates3, other3).astype(bf16))
    return out.at[0].set(from_prev)


def solution(mesh):
    return jax.shard_map(
        on_device,
        mesh=mesh,
        in_specs=(
            P("blk", None, "tp"),
            P("blk", None, "tp"),
            P("blk", None, "tp"),
            P("blk", None, "tp"),
            P("tp", None),
            P("blk"),
            P("blk", None),
            P("blk"),
            P("blk"),
        ),
        out_specs=P("blk", None, "tp"),
        check_vma=False,
    )
```

time: 59.1 us -> 66.1 us (1.12)
  Pallas kernels: 20.4 us -> 26.2 us
  starting transfers between devices: 13.2 us -> 15.1 us
  other arithmetic: 2.55 us -> 1.35 us
  local copies, waits for them, and re-layouts: 2.07 us -> 2.96 us
    pallas_call x2 -> x3, Pallas kernels: 20.4 us -> 26.2 us  [the longest x2 21.4 us: attend_blocks(): pl.pallas_call(functools.partial(attend_kernel, ids, shipped), grid_spec=...]
    ppermute x12, starting transfers between devices: 13.2 us -> 15.1 us  [the longest x4 5.19 us: sum_start(): return (got[0], lax.ppermute(across, 'tp', to_across))]
    convert_element_type x6 -> x5, other arithmetic: 2.25 us -> 0.99 us  [the longest x4 0.92 us: sum_start(): across = (keep.astype(wide) + got[1].astype(wide)).astype(bf16)]
    scatter x0 -> x4, local copies, waits for them, and re-layouts: none -> 0.98 us  [the longest x1 0.71 us: on_device(): return out.at[0].set(from_prev)]
    another operation x1 -> x0, local copies, waits for them, and re-layouts: 0.71 us -> none  [on_device(): return jnp.stack(from_prev + own + from_next)]
    unnamed x21 -> x4, local copies, waits for them, and re-layouts: 1.37 us -> 1.98 us
  transfers between devices with their start and end apart: 12 -> 12, of which waited for: 5 -> 2; matrix products, arithmetic and copies ran while one was open for 5% -> 2% of each run, Pallas kernels for 17% -> 29%
where the time goes in v3:
time: 66.1 us; the launch traced here: 65.8 us
  Pallas kernels  26.2 us (40%)
  waiting for transfers between devices  18.7 us (28%)
  starting transfers between devices  15.1 us (23%)
  local copies, waits for them, and re-layouts  2.96 us (4%)
  between operations  1.49 us (2%)
  other arithmetic  1.35 us (2%)
    pallas_call x2, Pallas kernels, attend_blocks(): pl.pallas_call(functools.partial(attend_kernel, ids, shipped), grid_spec=...  21.4 us
    ppermute x1, waiting for transfers between devices, on_device(): lax.ppermute(total(mine0, mates0, other0).astype(bf16), 'blk', to_prev)  11.3 us
    ppermute x1, waiting for transfers between devices, on_device(): moved = lax.ppermute(ship, 'blk', to_next)  7.46 us
    ppermute x4, starting transfers between devices, sum_start(): return (got[0], lax.ppermute(across, 'tp', to_across))  5.19 us
    pallas_call x1, Pallas kernels, project_block(): pl.pallas_call(project_kernel, in_specs=[anywhere] * 2, out_specs=[anywhe...  4.8 us
    ppermute x1, starting transfers between devices, on_device(): from_next1 = lax.ppermute(masked(result, 1 < left), 'blk', to_prev)  4.75 us
    ppermute x1, starting transfers between devices, on_device(): moved = lax.ppermute(ship, 'blk', to_next)  2.87 us
    unnamed x4, local copies, waits for them, and re-layouts  1.98 us
  transfers between devices with their start and end apart: 12, of which 2 were waited for; matrix products, arithmetic and copies ran while one was open for 2% of the time, Pallas kernels for 29%

profile of v3, /device:TPU:0, one launch (start us, length us, event | category | flops | bytes accessed | tf_op | source)
XLA Modules:
  0.0 65.8 jit_solution(2961057797127543621)
XLA Ops:
  0.0 7.0 %shard_map.92 = (bf16[2,128,896]{2,1,0:T(8,128)(2,1)S(1)}, bf16[128,896]{1,0:T(8,128)(2,1)S(1)}, f32[128,896]{1,0:T(8,128)S(1)}) custom-call(s32[4]{0:T(128)} %live_ref.3, bf16[4,128,896]{2,1,0:T(8,128)(2,1)} %q_hbm.3, bf16[4,2048,128]{2,1,0:T(8,128)(2,1)} %k_hbm.3, bf16[4,2048,128]{2,1,0:T(8,128)(2,1)} %v_hbm.3, bf16[4,128,896]{2,1,0:T(8,128)(2,1)} %hidden_hbm.3, ...), custom_call_target="tpu_custom_call" | custom-call | flops 1761607680 | bytes 7471104 | tf_op jit(solution)/shard_map/pallas_call | solution.py:281
  7.0 0.6 collective-permute-start.2
  7.5 14.4 %shard_map.91 = (bf16[2,128,896]{2,1,0:T(8,128)(2,1)S(1)}, bf16[2,128,896]{2,1,0:T(8,128)(2,1)S(1)}, bf16[128,896]{1,0:T(8,128)(2,1)S(1)}, bf16[128,896]{1,0:T(8...) custom-call(s32[4]{0:T(128)} %live_ref.3, ...), custom_call_target="tpu_custom_call" | custom-call | flops 4462739456 | bytes 9568256 | tf_op jit(solution)/shard_map/pallas_call | solution.py:281
  22.0 0.1 collective-permute-start
  22.1 0.5 collective-permute-start.4
  22.5 2.9 %collective-permute-start.8 = (bf16[2,128,896]{2,1,0:T(8,128)(2,1)}, bf16[2,128,896]{2,1,0:T(8,128)(2,1)S(1)}, u32[]{:S(2)}, u32[]{:S(2)}) collective-permute-start(bf16[2,128,896]{2,1,0:T(8,128)(2,1)} %get-tuple-element.99), channel_id=1, source_target_pairs={{0,4},{4,8},{8,12},{12,16},{16,20},{20,24},{24,28},{28,0},{1,5},{5... | collective-permute-start | bytes 1376264 | tf_op jit(solution)/shard_map/ppermute | solution.py:351
  26.7 0.0 collective-permute-done.2
  26.7 0.1 fusion.6
  26.8 1.6 %collective-permute-start.3 = (bf16[128,896]{1,0:T(8,128)(2,1)S(1)}, bf16[128,896]{1,0:T(8,128)(2,1)S(1)}, u32[]{:S(2)}, u32[]{:S(2)}) collective-permute-start(bf16[128,896]{1,0:T(8,128)(2,1)S(1)} %fusion.6), channel_id=1, source_target_pairs={{0,2},{1,3},{2,0},{3,1},{4,6},{5,7},{6,4},{7,5},{8,10},{9,11},{10,... | collective-permute-start | bytes 688136 | tf_op jit(solution)/shard_map/ppermute | solution.py:343
  28.4 0.0 collective-permute-done
  28.4 0.7 %fusion.9 = bf16[128,896]{1,0:T(8,128)(2,1)} fusion(bf16[128,896]{1,0:T(8,128)(2,1)S(1)} %get-tuple-element.92, bf16[2,128,896]{2,1,0:T(8,128)(2,1)S(1)} %collective-permute-done), kind=kLoop, calls=%fused_computation.16 | loop fusion | flops 458752 | bytes 688128 | tf_op jit(solution)/shard_map/convert_element_type | solution.py:342
  29.1 0.5 collective-permute-start.1
  29.6 0.0 collective-permute-done.4
  29.6 0.1 fusion.3
  29.7 1.6 %collective-permute-start.5 = (bf16[128,896]{1,0:T(8,128)(2,1)S(1)}, bf16[128,896]{1,0:T(8,128)(2,1)S(1)}, u32[]{:S(2)}, u32[]{:S(2)}) collective-permute-start(bf16[128,896]{1,0:T(8,128)(2,1)S(1)} %fusion.3), channel_id=1, source_target_pairs={{0,2},{1,3},{2,0},{3,1},{4,6},{5,7},{6,4},{7,5},{8,10},{9,11},{10,... | collective-permute-start | bytes 688136 | tf_op jit(solution)/shard_map/ppermute | solution.py:343
  31.3 7.5 %collective-permute-done.8.moved_hbm = bf16[2,128,896]{2,1,0:T(8,128)(2,1)S(1)} collective-permute-done((bf16[2,128,896]{2,1,0:T(8,128)(2,1)}, bf16[2,128,896]{2,1,0:T(8,128)(2,1)S(1)}, u32[]{:S(2)}, u32[]{:S(2)}) %collective-permute-start.8) | collective-permute-done | bytes 458784 | tf_op jit(solution)/shard_map/ppermute | solution.py:351
  38.7 0.0 copy-start.1
  38.7 0.8 %copy-done.1 = bf16[2,128,896]{2,1,0:T(8,128)(2,1)} copy-done((bf16[2,128,896]{2,1,0:T(8,128)(2,1)}, bf16[2,128,896]{2,1,0:T(8,128)(2,1)S(1)}, u32[]{:S(2)}) %copy-start.1) | copy-done | bytes 458776
  39.5 4.8 %shard_map.93 = (bf16[2,128,896]{2,1,0:T(8,128)(2,1)S(1)}, bf16[128,896]{1,0:T(8,128)(2,1)S(1)}, f32[128,896]{1,0:T(8,128)S(1)}) custom-call(bf16[2,128,896]{2,1,0:T(8,128)(2,1)} %copy-done.1, bf16[896,3584]{1,0:T(8,128)(2,1)} %w_hbm.5), custom_call_target="tpu_custom_call" | custom-call | flops 822083584 | bytes 6422528 | tf_op jit(solution)/shard_map/pallas_call | solution.py:299
  44.3 0.1 collective-permute-start.9
  44.4 0.0 collective-permute-done.3
  44.4 0.1 broadcast_select_fusion
  44.5 0.1 collective-permute-start.11
  44.5 0.0 collective-permute-done.1
  44.6 0.1 broadcast_select_fusion.1
  44.7 4.7 %collective-permute-start.7 = (bf16[128,896]{1,0:T(8,128)(2,1)S(1)}, bf16[128,896]{1,0:T(8,128)(2,1)S(1)}, u32[]{:S(2)}, u32[]{:S(2)}) collective-permute-start(bf16[128,896]{1,0:T(8,128)(2,1)S(1)} %get-tuple-element.105), channel_id=1, source_target_pairs={{0,28},{4,0},{8,4},{12,8},{16,12},{20,16},{24,20},{28,24},{1,29},{... | collective-permute-start | bytes 688136 | tf_op jit(solution)/shard_map/ppermute | solution.py:365
  49.4 0.0 collective-permute-done.5
  49.4 0.1 fusion.5
  49.5 1.0 %collective-permute-start.6 = (bf16[128,896]{1,0:T(8,128)(2,1)S(1)}, bf16[128,896]{1,0:T(8,128)(2,1)S(1)}, u32[]{:S(2)}, u32[]{:S(2)}) collective-permute-start(bf16[128,896]{1,0:T(8,128)(2,1)S(1)} %fusion.5), channel_id=1, source_target_pairs={{0,28},{4,0},{8,4},{12,8},{16,12},{20,16},{24,20},{28,24},{1,29},{... | collective-permute-start | bytes 688136 | tf_op jit(solution)/shard_map/ppermute | solution.py:362
  50.5 0.2 scatter.20
  50.8 0.1 bitcast_dynamic-update-slice_fusion.3
  50.8 0.0 collective-permute-done.9
  50.8 0.1 fusion
  50.9 1.5 %collective-permute-start.10 = (bf16[128,896]{1,0:T(8,128)(2,1)S(1)}, bf16[128,896]{1,0:T(8,128)(2,1)S(1)}, u32[]{:S(2)}, u32[]{:S(2)}) collective-permute-start(bf16[128,896]{1,0:T(8,128)(2,1)S(1)} %fusion), channel_id=1, source_target_pairs={{0,2},{1,3},{2,0},{3,1},{4,6},{5,7},{6,4},{7,5},{8,10},{9,11},{10,... | collective-permute-start | bytes 688136 | tf_op jit(solution)/shard_map/ppermute | solution.py:343
  52.4 11.3 %collective-permute-done.6 = bf16[128,896]{1,0:T(8,128)(2,1)S(1)} collective-permute-done((bf16[128,896]{1,0:T(8,128)(2,1)S(1)}, bf16[128,896]{1,0:T(8,128)(2,1)S(1)}, u32[]{:S(2)}, u32[]{:S(2)}) %collective-permute-start.6) | collective-permute-done | bytes 229408 | tf_op jit(solution)/shard_map/ppermute | solution.py:362
  63.7 0.0 collective-permute-done.7
  63.8 0.0 collective-permute-done.10
  63.8 0.1 fusion.13
  63.9 0.0 copy-start
  63.9 0.0 collective-permute-done.11
  63.9 1.2 %copy-done = bf16[8,128,896]{2,1,0:T(8,128)(2,1)} copy-done((bf16[8,128,896]{2,1,0:T(8,128)(2,1)}, bf16[8,128,896]{2,1,0:T(8,128)(2,1)S(1)}, u32[]{:S(2)}) %copy-start) | copy-done | bytes 1835032
  65.1 0.7 %bitcast_dynamic-update-slice_fusion = bf16[8,128,896]{2,1,0:T(8,128)(2,1)} fusion(bf16[8,128,896]{2,1,0:T(8,128)(2,1)} %copy-done, bf16[128,896]{1,0:T(8,128)(2,1)S(1)} %collective-permute-done.11), kind=kLoop, calls=%fused_computation.30 | loop fusion | bytes 458752 | tf_op jit(solution)/shard_map/scatter | solution.py:374
  (3 shorter events, 0.1 us)
Async XLA Ops:
  7.0 19.7 %collective-permute-start.2 = (bf16[2,128,896]{2,1,0:T(8,128)(2,1)S(1)}, bf16[2,128,896]{2,1,0:T(8,128)(2,1)S(1)}, u32[]{:S(2)}, u32[]{:S(2)}) collective-permute-start(bf16[2,128,896]{2,1,0:T(8,128)(2,1)S(1)} %get-tuple-element.94), channel_id=1, source_target_pairs={{0,1},{1,0},{2,3},{3,2},{4,5},{5,4},{6,7},{7,6},{8,9},{9,8},{10,11... | collective-permute-start | bytes 1376264 | tf_op jit(solution)/shard_map/ppermute | solution.py:341
  22.0 6.4 %collective-permute-start = (bf16[2,128,896]{2,1,0:T(8,128)(2,1)S(1)}, bf16[2,128,896]{2,1,0:T(8,128)(2,1)S(1)}, u32[]{:S(2)}, u32[]{:S(2)}) collective-permute-start(bf16[2,128,896]{2,1,0:T(8,128)(2,1)S(1)} %get-tuple-element.91), channel_id=1, source_target_pairs={{0,1},{1,0},{2,3},{3,2},{4,5},{5,4},{6,7},{7,6},{8,9},{9,8},{10,11... | collective-permute-start | bytes 1376264 | tf_op jit(solution)/shard_map/ppermute | solution.py:341
  22.1 7.6 %collective-permute-start.4 = (bf16[2,128,896]{2,1,0:T(8,128)(2,1)S(1)}, bf16[2,128,896]{2,1,0:T(8,128)(2,1)S(1)}, u32[]{:S(2)}, u32[]{:S(2)}) collective-permute-start(bf16[2,128,896]{2,1,0:T(8,128)(2,1)S(1)} %get-tuple-element.97), channel_id=1, source_target_pairs={{0,1},{1,0},{2,3},{3,2},{4,5},{5,4},{6,7},{7,6},{8,9},{9,8},{10,11... | collective-permute-start | bytes 1376264 | tf_op jit(solution)/shard_map/ppermute | solution.py:341
  22.5 16.2 %collective-permute-start.8 = (bf16[2,128,896]{2,1,0:T(8,128)(2,1)}, bf16[2,128,896]{2,1,0:T(8,128)(2,1)S(1)}, u32[]{:S(2)}, u32[]{:S(2)}) collective-permute-start(bf16[2,128,896]{2,1,0:T(8,128)(2,1)} %get-tuple-element.99), channel_id=1, source_target_pairs={{0,4},{4,8},{8,12},{12,16},{16,20},{20,24},{24,28},{28,0},{1,5},{5... | collective-permute-start | bytes 1376264 | tf_op jit(solution)/shard_map/ppermute | solution.py:351
  26.8 17.6 %collective-permute-start.3 = (bf16[128,896]{1,0:T(8,128)(2,1)S(1)}, bf16[128,896]{1,0:T(8,128)(2,1)S(1)}, u32[]{:S(2)}, u32[]{:S(2)}) collective-permute-start(bf16[128,896]{1,0:T(8,128)(2,1)S(1)} %fusion.6), channel_id=1, source_target_pairs={{0,2},{1,3},{2,0},{3,1},{4,6},{5,7},{6,4},{7,5},{8,10},{9,11},{10,... | collective-permute-start | bytes 688136 | tf_op jit(solution)/shard_map/ppermute | solution.py:343
  29.1 15.4 %collective-permute-start.1 = (bf16[128,896]{1,0:T(8,128)(2,1)}, bf16[128,896]{1,0:T(8,128)(2,1)S(1)}, u32[]{:S(2)}, u32[]{:S(2)}) collective-permute-start(bf16[128,896]{1,0:T(8,128)(2,1)} %fusion.9), channel_id=1, source_target_pairs={{0,2},{1,3},{2,0},{3,1},{4,6},{5,7},{6,4},{7,5},{8,10},{9,11},{10,... | collective-permute-start | bytes 688136 | tf_op jit(solution)/shard_map/ppermute | solution.py:343
  29.7 19.7 %collective-permute-start.5 = (bf16[128,896]{1,0:T(8,128)(2,1)S(1)}, bf16[128,896]{1,0:T(8,128)(2,1)S(1)}, u32[]{:S(2)}, u32[]{:S(2)}) collective-permute-start(bf16[128,896]{1,0:T(8,128)(2,1)S(1)} %fusion.3), channel_id=1, source_target_pairs={{0,2},{1,3},{2,0},{3,1},{4,6},{5,7},{6,4},{7,5},{8,10},{9,11},{10,... | collective-permute-start | bytes 688136 | tf_op jit(solution)/shard_map/ppermute | solution.py:343
  38.7 0.8 %copy-start.1 = (bf16[2,128,896]{2,1,0:T(8,128)(2,1)}, bf16[2,128,896]{2,1,0:T(8,128)(2,1)S(1)}, u32[]{:S(2)}) copy-start(bf16[2,128,896]{2,1,0:T(8,128)(2,1)S(1)} %collective-permute-done.8.moved_hbm) | copy-start | bytes 1376260
  44.3 6.5 %collective-permute-start.9 = (bf16[2,128,896]{2,1,0:T(8,128)(2,1)S(1)}, bf16[2,128,896]{2,1,0:T(8,128)(2,1)S(1)}, u32[]{:S(2)}, u32[]{:S(2)}) collective-permute-start(bf16[2,128,896]{2,1,0:T(8,128)(2,1)S(1)} %get-tuple-element.101), channel_id=1, source_target_pairs={{0,1},{1,0},{2,3},{3,2},{4,5},{5,4},{6,7},{7,6},{8,9},{9,8},{10,11... | collective-permute-start | bytes 1376264 | tf_op jit(solution)/shard_map/ppermute | solution.py:341
  44.5 19.4 %collective-permute-start.11 = (bf16[128,896]{1,0:T(8,128)(2,1)S(1)}, bf16[128,896]{1,0:T(8,128)(2,1)S(1)}, u32[]{:S(2)}, u32[]{:S(2)}) collective-permute-start(bf16[128,896]{1,0:T(8,128)(2,1)S(1)} %get-tuple-element.103), channel_id=1, source_target_pairs={{0,4},{4,8},{8,12},{12,16},{16,20},{20,24},{24,28},{28,0},{1,5},{5... | collective-permute-start | bytes 688136 | tf_op jit(solution)/shard_map/ppermute | solution.py:368
  44.7 19.1 %collective-permute-start.7 = (bf16[128,896]{1,0:T(8,128)(2,1)S(1)}, bf16[128,896]{1,0:T(8,128)(2,1)S(1)}, u32[]{:S(2)}, u32[]{:S(2)}) collective-permute-start(bf16[128,896]{1,0:T(8,128)(2,1)S(1)} %get-tuple-element.105), channel_id=1, source_target_pairs={{0,28},{4,0},{8,4},{12,8},{16,12},{20,16},{24,20},{28,24},{1,29},{... | collective-permute-start | bytes 688136 | tf_op jit(solution)/shard_map/ppermute | solution.py:365
  49.5 14.2 %collective-permute-start.6 = (bf16[128,896]{1,0:T(8,128)(2,1)S(1)}, bf16[128,896]{1,0:T(8,128)(2,1)S(1)}, u32[]{:S(2)}, u32[]{:S(2)}) collective-permute-start(bf16[128,896]{1,0:T(8,128)(2,1)S(1)} %fusion.5), channel_id=1, source_target_pairs={{0,28},{4,0},{8,4},{12,8},{16,12},{20,16},{24,20},{28,24},{1,29},{... | collective-permute-start | bytes 688136 | tf_op jit(solution)/shard_map/ppermute | solution.py:362
  50.9 12.9 %collective-permute-start.10 = (bf16[128,896]{1,0:T(8,128)(2,1)S(1)}, bf16[128,896]{1,0:T(8,128)(2,1)S(1)}, u32[]{:S(2)}, u32[]{:S(2)}) collective-permute-start(bf16[128,896]{1,0:T(8,128)(2,1)S(1)} %fusion), channel_id=1, source_target_pairs={{0,2},{1,3},{2,0},{3,1},{4,6},{5,7},{6,4},{7,5},{8,10},{9,11},{10,... | collective-permute-start | bytes 688136 | tf_op jit(solution)/shard_map/ppermute | solution.py:343
  63.9 1.2 %copy-start = (bf16[8,128,896]{2,1,0:T(8,128)(2,1)}, bf16[8,128,896]{2,1,0:T(8,128)(2,1)S(1)}, u32[]{:S(2)}) copy-start(bf16[8,128,896]{2,1,0:T(8,128)(2,1)S(1)} %fusion.13) | copy-start | bytes 5505028

commit v4 on v3

--- a/solution.py
+++ b/solution.py
@@ -14,7 +14,7 @@
 SEG = 512
 LOG2E = 1.4426950408889634
 MASKED = -1e30
-VMEM_LIMIT = 58 << 20
+VMEM_LIMIT = 44 << 20
 
 
 def group_softmax(n, qg, kx_ref, vx_ref, b, scale, hd):
@@ -52,41 +52,35 @@
     return copies
 
 
-def project(attn, residual, w_ref, w_copies, part_ref, mine_ref, outs, sems):
-    count, cols = len(outs) // 3, mine_ref.shape[1]
-    nodes = attn.shape[0] // count
-    copies = [[] for _ in range(4)]
-    for b in range(count):
-        at = pl.ds(b * nodes, nodes)
-        to = [outs[b].at[0], outs[b].at[1], outs[count + b]]
-        for s in range(3):
-            copies[s].append(pltpu.make_async_copy(part_ref.at[s, at], to[s], sems.at[b, s]))
-        copies[3].append(pltpu.make_async_copy(mine_ref.at[at], outs[2 * count + b], sems.at[b, 3]))
-    w_copies[0].wait()
-    w_copies[1].wait()
+def project(attn, residual, w_ref, w_copies, outs):
+    count = len(outs) // 3
+    nodes, cols = outs[-1].shape
+    for copy in w_copies[:2]:
+        copy.wait()
     part = jnp.dot(attn, w_ref[0], preferred_element_type=jnp.float32)
-    for s in range(2):
-        part_ref[s] = part[:, s * cols : (s + 1) * cols].astype(jnp.bfloat16)
-        for copy in copies[s]:
-            copy.start()
-    w_copies[2].wait()
-    w_copies[3].wait()
+    for b in range(count):
+        at = slice(b * nodes, (b + 1) * nodes)
+        for s in range(2):
+            outs[b][s] = part[at, s * cols : (s + 1) * cols].astype(jnp.bfloat16)
+    for copy in w_copies[2:]:
+        copy.wait()
     part = jnp.dot(attn, w_ref[1], preferred_element_type=jnp.float32)
-    part_ref[2] = part[:, :cols].astype(jnp.bfloat16)
-    mine_ref[...] = part[:, cols:] + residual().astype(jnp.float32)
-    for copy in copies[2] + copies[3]:
-        copy.start()
-    return sum(copies, [])
+    rest = residual().astype(jnp.float32)
+    for b in range(count):
+        at = slice(b * nodes, (b + 1) * nodes)
+        outs[count + b][...] = part[at, :cols].astype(jnp.bfloat16)
+        outs[2 * count + b][...] = part[at, cols:] + rest[at]
 
 
 def attend_kernel(
     ids, shipped, live_ref, q_hbm, k_hbm, v_hbm, hidden_hbm, tiles_hbm, w_hbm, *refs,
 ):
     made = len(ids) - shipped
-    outs, refs = refs[: 3 * made + shipped], refs[3 * made + shipped :]
+    extra = 2 if shipped else 0
+    outs, refs = refs[: 3 * made + extra], refs[3 * made + extra :]
     (
-        tiles_ref, hidden_ref, ship_ref, q_ref, w_ref, kx_ref, vx_ref, qx_ref, attn_ref, perm_ref,
-        part_ref, mine_ref, segs_ref, sems, out_sems,
+        tiles_ref, hidden_ref, q_ref, kx_ref, vx_ref, qx_ref, attn_ref, perm_ref,
+        segs_ref, sems,
     ) = refs
     count, nodes, width = q_ref.shape
     places, hd = kx_ref.shape[1], kx_ref.shape[2] // 2
@@ -107,7 +101,8 @@
         )
         into = hidden_ref.at[pl.ds(b * nodes, nodes)]
         hidden_copies.append(pltpu.make_async_copy(hidden_hbm.at[j], into, sems.at[6, b]))
-    w_copies = weight_copies(w_hbm, w_ref, sems.at[4])
+    w_ref = outs[3 * made + 1] if shipped else w_hbm
+    w_copies = weight_copies(w_hbm, w_ref, sems.at[4]) if shipped else []
     tiles_copy.start()
     for b in range(count):
         q_copies[b].start()
@@ -163,7 +158,6 @@
         residual = hidden_ref[b * nodes : (b + 1) * nodes, :]
         return jnp.where(row < live_ref[ids[b]], residual, jnp.zeros((), residual.dtype))
 
-    ship_copies = []
     for b, j in enumerate(ids):
         k_copies[b].wait()
         v_copies[b].wait()
@@ -197,11 +191,9 @@
             perm_ref[b], attn_ref[at, :], preferred_element_type=jnp.float32
         ).astype(jnp.bfloat16)
         if b < shipped:
-            ship_ref[0] = in_place
+            outs[3 * made][0] = in_place
             hidden_copies[b].wait()
-            ship_ref[1] = alive_residual(b)
-            ship_copies.append(pltpu.make_async_copy(ship_ref, outs[3 * made], sems.at[3, 1]))
-            ship_copies[0].start()
+            outs[3 * made][1] = alive_residual(b)
         else:
             attn_ref[at, :] = in_place
 
@@ -210,30 +202,11 @@
             copy.wait()
         return jnp.concatenate([alive_residual(b) for b in range(shipped, count)], axis=0)
 
-    out_copies = project(
-        attn_ref[shipped * nodes :, :], residual, w_ref, w_copies, part_ref, mine_ref,
-        outs[: 3 * made], out_sems,
-    )
-    for copy in ship_copies + out_copies:
-        copy.wait()
-
-
-def project_kernel(
-    moved_hbm, w_hbm, send_hbm, keep_hbm, mine_hbm, moved_ref, w_ref, part_ref, mine_ref, sems,
-    out_sems,
-):
-    moved_copy = pltpu.make_async_copy(moved_hbm, moved_ref, sems.at[2, 0])
-    moved_copy.start()
-    w_copies = weight_copies(w_hbm, w_ref, sems.at[0])
-    for copy in w_copies:
-        copy.start()
-    moved_copy.wait()
-    out_copies = project(
-        moved_ref[0], lambda: moved_ref[1], w_ref, w_copies, part_ref, mine_ref,
-        (send_hbm, keep_hbm, mine_hbm), out_sems,
-    )
-    for copy in out_copies:
-        copy.wait()
+    project(attn_ref[shipped * nodes :, :], residual, w_ref, w_copies, outs[: 3 * made])
+
+
+def project_kernel(moved_ref, w_ref, *outs):
+    project(moved_ref[0], lambda: moved_ref[1], w_ref, [], outs)
 
 
 def partial_shapes(count, rows, cols):
@@ -253,29 +226,26 @@
     made = (count - shipped) * nodes
     bf16 = jnp.bfloat16
     outs = partial_shapes(count - shipped, nodes, cols)
-    outs += [jax.ShapeDtypeStruct((2, nodes, cols), bf16)] * shipped
+    in_vmem = pl.BlockSpec(memory_space=pltpu.VMEM)
+    if shipped:
+        outs += [pltpu.VMEM((2, nodes, cols), bf16), pltpu.VMEM((2, width, 2 * cols), bf16)]
     anywhere = pl.BlockSpec(memory_space=pl.ANY)
     grid_spec = pltpu.PrefetchScalarGridSpec(
         num_scalar_prefetch=1,
-        grid=(1,),
-        in_specs=[anywhere] * 6,
-        out_specs=[anywhere] * len(outs),
+        grid=(),
+        in_specs=[anywhere] * 5 + [anywhere if shipped else in_vmem],
+        out_specs=[in_vmem] * len(outs),
         scratch_shapes=[
             pltpu.VMEM(tiles.shape, jnp.int32),
             pltpu.VMEM((count * nodes, cols), bf16),
-            pltpu.VMEM((2, nodes, cols), bf16),
             pltpu.VMEM((count, nodes, width), bf16),
-            pltpu.VMEM((2, width, 2 * cols), bf16),
             pltpu.VMEM((count, places, 2 * hd), bf16),
             pltpu.VMEM((count, places, 2 * hd), bf16),
             pltpu.VMEM((count * heads * nodes, 2 * hd), bf16),
             pltpu.VMEM((count * nodes, width), bf16),
             pltpu.VMEM((count, nodes, nodes), bf16),
-            pltpu.VMEM((3, made, cols), bf16),
-            pltpu.VMEM((made, cols), jnp.float32),
             pltpu.SMEM((count * (nodes // GROUP),), jnp.int32),
             pltpu.SemaphoreType.DMA((7, max(4, count))),
-            pltpu.SemaphoreType.DMA((count - shipped, 4)),
         ],
     )
     return pl.pallas_call(
@@ -284,7 +254,7 @@
         out_shape=outs,
         compiler_params=pltpu.CompilerParams(vmem_limit_bytes=VMEM_LIMIT),
         cost_estimate=pl.CostEstimate(
-            flops=4 * count * nodes * width * places + 2 * made * width * w.shape[1],
+            flops=4 * count * nodes * width * places + 8 * made * width * cols,
             bytes_accessed=w.size * 2 + count * 4 * places * hd,
             transcendentals=count * nodes * heads * places,
         ),
@@ -293,25 +263,16 @@
 
 def project_block(moved, w):
     _, nodes, cols = moved.shape
-    width = w.shape[0]
     outs = partial_shapes(1, nodes, cols)
-    anywhere = pl.BlockSpec(memory_space=pl.ANY)
+    in_vmem = pl.BlockSpec(memory_space=pltpu.VMEM)
     return pl.pallas_call(
         project_kernel,
-        in_specs=[anywhere] * 2,
-        out_specs=[anywhere] * len(outs),
-        scratch_shapes=[
-            pltpu.VMEM(moved.shape, jnp.bfloat16),
-            pltpu.VMEM((2, width, 2 * cols), jnp.bfloat16),
-            pltpu.VMEM((3, nodes, cols), jnp.bfloat16),
-            pltpu.VMEM((nodes, cols), jnp.float32),
-            pltpu.SemaphoreType.DMA((3, 4)),
-            pltpu.SemaphoreType.DMA((1, 4)),
-        ],
+        in_specs=[in_vmem] * 2,
+        out_specs=[in_vmem] * len(outs),
         out_shape=outs,
         compiler_params=pltpu.CompilerParams(vmem_limit_bytes=VMEM_LIMIT),
         cost_estimate=pl.CostEstimate(
-            flops=2 * nodes * width * w.shape[1], bytes_accessed=w.size * 2, transcendentals=0
+            flops=2 * nodes * w.size * 2, bytes_accessed=w.size * 2, transcendentals=0
         ),
     )(moved, w)
 
@@ -331,10 +292,15 @@
     left, right = left_count[0], right_count[0]
     zero = jnp.zeros((), jnp.bfloat16)
 
-    def attend(ids, shipped):
+    in_hbm = [kv_keys, kv_values, queries, hidden, out_weight, node_tiles]
+    kv_keys, kv_values, queries, hidden, out_weight, node_tiles = [
+        pltpu.with_memory_space_constraint(a, pltpu.HBM) for a in in_hbm
+    ]
+
+    def attend(ids, shipped, weight):
         return attend_blocks(
             ids, shipped, queries, kv_keys, kv_values, hidden, node_tiles, block_live,
-            out_weight,
+            weight,
         )
 
     def sum_start(send, keep):
@@ -347,13 +313,13 @@
 
     last = blocks - 1
     out = jnp.zeros((blocks + 2 * S_MAX, nodes, hidden.shape[2]), bf16)
-    send0, send1, keep0, keep1, mine0, mine1, ship = attend((last, 0, 1), 1)
+    send0, send1, keep0, keep1, mine0, mine1, ship, weight = attend((last, 0, 1), 1, out_weight)
     moved = lax.ppermute(ship, "blk", to_next)
     mates0, other0 = sum_start(send0, keep0)
     mates1, other1 = sum_start(send1, keep1)
-    send2, keep2, mine2 = attend((2,), 0)
+    send2, keep2, mine2 = attend((2,), 0, weight)
     mates2, other2 = sum_start(send2, keep2)
-    send3, keep3, mine3 = project_block(moved, out_weight)
+    send3, keep3, mine3 = project_block(moved, weight)
     mates3, other3 = sum_start(send3, keep3)
 
     def masked(value, kept):

time: 66.1 us -> 54.5 us (0.82)
  Pallas kernels: 26.2 us -> 18.4 us
  waiting for transfers between devices: 18.7 us -> 12.5 us
  starting transfers between devices: 15.1 us -> 18.4 us
  other arithmetic: 1.35 us -> 0.67 us
    ppermute x1, waiting for transfers between devices: 11.3 us -> 3.61 us  [on_device(): lax.ppermute(total(mine0, mates0, other0).astype(bf16), 'blk', to_prev)]
    ppermute x1, starting transfers between devices: 0.06 us -> 4.53 us  [on_device(): lax.ppermute(masked(result, blocks - 2 <= right), 'blk', to_next)]
    ppermute x4, waiting for transfers between devices: 0.01 us -> 4.22 us  [sum_start(): return (got[0], lax.ppermute(across, 'tp', to_across))]
    pallas_call x2, Pallas kernels: 21.4 us -> 17.2 us  [attend_blocks(): pl.pallas_call(functools.partial(attend_kernel, ids, shipped), grid_spec=...]
    pallas_call x1, Pallas kernels: 4.8 us -> 1.17 us  [project_block(): pl.pallas_call(project_kernel, in_specs=[in_vmem] * 2, out_specs=[in_vmem...]
    ppermute x1, starting transfers between devices: 4.75 us -> 1.48 us  [on_device(): from_next1 = lax.ppermute(masked(result, 1 < left), 'blk', to_prev)]
    ppermute x1, waiting for transfers between devices: 7.46 us -> 4.63 us  [on_device(): moved = lax.ppermute(ship, 'blk', to_next)]
    ppermute x1, starting transfers between devices: 1.01 us -> 3.34 us  [on_device(): lax.ppermute(total(mine0, mates0, other0).astype(bf16), 'blk', to_prev)]
  transfers between devices with their start and end apart: 12 -> 12, of which waited for: 2 -> 5; matrix products, arithmetic and copies ran while one was open for 2% -> 2% of each run, Pallas kernels for 29% -> 12%
where the time goes in v4:
time: 54.5 us; the launch traced here: 54.2 us
  Pallas kernels  18.4 us (34%)
  starting transfers between devices  18.4 us (34%)
  waiting for transfers between devices  12.5 us (23%)
  local copies, waits for them, and re-layouts  2.85 us (5%)
  between operations  1.47 us (3%)
  other arithmetic  0.67 us (1%)
    pallas_call x2, Pallas kernels, attend_blocks(): pl.pallas_call(functools.partial(attend_kernel, ids, shipped), grid_spec=...  17.2 us
    ppermute x4, starting transfers between devices, sum_start(): return (got[0], lax.ppermute(across, 'tp', to_across))  5.92 us
    ppermute x1, waiting for transfers between devices, on_device(): moved = lax.ppermute(ship, 'blk', to_next)  4.63 us
    ppermute x1, starting transfers between devices, on_device(): lax.ppermute(masked(result, blocks - 2 <= right), 'blk', to_next)  4.53 us
    ppermute x4, waiting for transfers between devices, sum_start(): return (got[0], lax.ppermute(across, 'tp', to_across))  4.22 us
    ppermute x1, waiting for transfers between devices, on_device(): lax.ppermute(total(mine0, mates0, other0).astype(bf16), 'blk', to_prev)  3.61 us
    ppermute x1, starting transfers between devices, on_device(): lax.ppermute(total(mine0, mates0, other0).astype(bf16), 'blk', to_prev)  3.34 us
    ppermute x1, starting transfers between devices, on_device(): moved = lax.ppermute(ship, 'blk', to_next)  2.33 us
  transfers between devices with their start and end apart: 12, of which 5 were waited for; matrix products, arithmetic and copies ran while one was open for 2% of the time, Pallas kernels for 12%

profile of v4, /device:TPU:0, one launch (start us, length us, event | category | flops | bytes accessed | tf_op | source)
XLA Modules:
  0.0 54.2 jit_solution(7357194192310002639)
XLA Ops:
  0.0 0.0 copy-start
  0.0 0.7 %copy-done = s32[4]{0:T(128)S(1)} copy-done((s32[4]{0:T(128)S(1)}, s32[4]{0:T(128)}, u32[]{:S(2)}) %copy-start) | copy-done | bytes 40
  0.7 11.9 %shard_map.91 = (bf16[2,128,896]{2,1,0:T(8,128)(2,1)S(1)}, bf16[2,128,896]{2,1,0:T(8,128)(2,1)S(1)}, bf16[128,896]{1,0:T(8,128)(2,1)S(1)}, bf16[128,896]{1,0:T(8...) custom-call(s32[4]{0:T(128)S(1)} %copy-done, ...), custom_call_target="tpu_custom_call" | custom-call | flops 4462739456 | bytes 9568256 | tf_op jit(solution)/shard_map/pallas_call | solution.py:251
  12.6 0.6 %collective-permute-start = (bf16[2,128,896]{2,1,0:T(8,128)(2,1)S(1)}, bf16[2,128,896]{2,1,0:T(8,128)(2,1)S(1)}, u32[]{:S(2)}, u32[]{:S(2)}) collective-permute-start(bf16[2,128,896]{2,1,0:T(8,128)(2,1)S(1)} %get-tuple-element.92), channel_id=1, source_target_pairs={{0,1},{1,0},{2,3},{3,2},{4,5},{5,4},{6,7},{7,6},{8,9},{9,8},{10,11... | collective-permute-start | bytes 1376264 | tf_op jit(solution)/shard_map/ppermute | solution.py:307
  13.2 0.1 collective-permute-start.4
  13.2 2.3 %collective-permute-start.8 = (bf16[2,128,896]{2,1,0:T(8,128)(2,1)S(1)}, bf16[2,128,896]{2,1,0:T(8,128)(2,1)S(1)}, u32[]{:S(2)}, u32[]{:S(2)}) collective-permute-start(bf16[2,128,896]{2,1,0:T(8,128)(2,1)S(1)} %get-tuple-element.101), channel_id=1, source_target_pairs={{0,4},{4,8},{8,12},{12,16},{16,20},{20,24},{24,28},{28,0},{1,5},{5... | collective-permute-start | bytes 1376264 | tf_op jit(solution)/shard_map/ppermute | solution.py:317
  15.6 5.3 %shard_map.92 = (bf16[2,128,896]{2,1,0:T(8,128)(2,1)S(1)}, bf16[128,896]{1,0:T(8,128)(2,1)S(1)}, f32[128,896]{1,0:T(8,128)S(1)}) custom-call(s32[4]{0:T(128)S(1)} %copy-done, bf16[4,128,896]{2,1,0:T(8,128)(2,1)} %q_hbm.3, bf16[4,2048,128]{2,1,0:T(8,128)(2,1)} %k_hbm.3, bf16[4,2048,128]{2,1,0:T(8,128)(2,1)} %v_hbm.3, bf16[4,128,896]{2,1,0:T(8,128)(2,1)} %hidden_hbm.3, ...), custom_call_target="tpu_custom_call" | custom-call | flops 1761607680 | bytes 7471104 | tf_op jit(solution)/shard_map/pallas_call | solution.py:251
  20.9 0.1 collective-permute-start.2
  22.3 0.0 collective-permute-done
  22.3 0.1 fusion.9
  22.3 1.6 %collective-permute-start.1 = (bf16[128,896]{1,0:T(8,128)(2,1)S(1)}, bf16[128,896]{1,0:T(8,128)(2,1)S(1)}, u32[]{:S(2)}, u32[]{:S(2)}) collective-permute-start(bf16[128,896]{1,0:T(8,128)(2,1)S(1)} %fusion.9), channel_id=1, source_target_pairs={{0,2},{1,3},{2,0},{3,1},{4,6},{5,7},{6,4},{7,5},{8,10},{9,11},{10,... | collective-permute-start | bytes 688136 | tf_op jit(solution)/shard_map/ppermute | solution.py:309
  23.9 0.0 collective-permute-done.4
  23.9 0.1 fusion.3
  24.0 0.6 %collective-permute-start.5 = (bf16[128,896]{1,0:T(8,128)(2,1)S(1)}, bf16[128,896]{1,0:T(8,128)(2,1)S(1)}, u32[]{:S(2)}, u32[]{:S(2)}) collective-permute-start(bf16[128,896]{1,0:T(8,128)(2,1)S(1)} %fusion.3), channel_id=1, source_target_pairs={{0,2},{1,3},{2,0},{3,1},{4,6},{5,7},{6,4},{7,5},{8,10},{9,11},{10,... | collective-permute-start | bytes 688136 | tf_op jit(solution)/shard_map/ppermute | solution.py:309
  24.6 4.6 %collective-permute-done.8.moved_ref = bf16[2,128,896]{2,1,0:T(8,128)(2,1)S(1)} collective-permute-done((bf16[2,128,896]{2,1,0:T(8,128)(2,1)S(1)}, bf16[2,128,896]{2,1,0:T(8,128)(2,1)S(1)}, u32[]{:S(2)}, u32[]{:S(2)}) %collective-permute-start.8) | collective-permute-done | bytes 458784 | tf_op jit(solution)/shard_map/ppermute | solution.py:317
  29.2 1.2 %shard_map.93 = (bf16[2,128,896]{2,1,0:T(8,128)(2,1)S(1)}, bf16[128,896]{1,0:T(8,128)(2,1)S(1)}, f32[128,896]{1,0:T(8,128)S(1)}) custom-call(bf16[2,128,896]{2,1,0:T(8,128)(2,1)S(1)} %collective-permute-done.8.moved_ref, bf16[2,896,1792]{2,1,0:T(8,128)(2,1)S(1)} %get-tuple-element.94.w_hbm.w_ref), custom_call_target="tpu_custom_call" | custom-call | flops 1644167168 | bytes 6422528 | tf_op jit(solution)/shard_map/pallas_call | solution.py:268
  30.4 0.1 collective-permute-start.9
  30.4 0.0 collective-permute-done.2
  30.5 0.1 fusion.6
  30.5 2.2 %collective-permute-start.3 = (bf16[128,896]{1,0:T(8,128)(2,1)S(1)}, bf16[128,896]{1,0:T(8,128)(2,1)S(1)}, u32[]{:S(2)}, u32[]{:S(2)}) collective-permute-start(bf16[128,896]{1,0:T(8,128)(2,1)S(1)} %fusion.6), channel_id=1, source_target_pairs={{0,2},{1,3},{2,0},{3,1},{4,6},{5,7},{6,4},{7,5},{8,10},{9,11},{10,... | collective-permute-start | bytes 688136 | tf_op jit(solution)/shard_map/ppermute | solution.py:309
  32.7 0.0 collective-permute-done.1
  32.7 0.1 broadcast_select_fusion.1
  32.8 1.5 %collective-permute-start.7 = (bf16[128,896]{1,0:T(8,128)(2,1)S(1)}, bf16[128,896]{1,0:T(8,128)(2,1)S(1)}, u32[]{:S(2)}, u32[]{:S(2)}) collective-permute-start(bf16[128,896]{1,0:T(8,128)(2,1)S(1)} %get-tuple-element.107), channel_id=1, source_target_pairs={{0,28},{4,0},{8,4},{12,8},{16,12},{20,16},{24,20},{28,24},{1,29},{... | collective-permute-start | bytes 688136 | tf_op jit(solution)/shard_map/ppermute | solution.py:331
  34.3 1.5 %collective-permute-done.5 = bf16[128,896]{1,0:T(8,128)(2,1)S(1)} collective-permute-done((bf16[128,896]{1,0:T(8,128)(2,1)S(1)}, bf16[128,896]{1,0:T(8,128)(2,1)S(1)}, u32[]{:S(2)}, u32[]{:S(2)}) %collective-permute-start.5) | collective-permute-done | bytes 229408 | tf_op jit(solution)/shard_map/ppermute | solution.py:309
  35.8 0.1 fusion.5
  35.9 3.3 %collective-permute-start.6 = (bf16[128,896]{1,0:T(8,128)(2,1)S(1)}, bf16[128,896]{1,0:T(8,128)(2,1)S(1)}, u32[]{:S(2)}, u32[]{:S(2)}) collective-permute-start(bf16[128,896]{1,0:T(8,128)(2,1)S(1)} %fusion.5), channel_id=1, source_target_pairs={{0,28},{4,0},{8,4},{12,8},{16,12},{20,16},{24,20},{28,24},{1,29},{... | collective-permute-start | bytes 688136 | tf_op jit(solution)/shard_map/ppermute | solution.py:328
  39.2 1.0 %collective-permute-done.3 = bf16[128,896]{1,0:T(8,128)(2,1)S(1)} collective-permute-done((bf16[128,896]{1,0:T(8,128)(2,1)S(1)}, bf16[128,896]{1,0:T(8,128)(2,1)S(1)}, u32[]{:S(2)}, u32[]{:S(2)}) %collective-permute-start.3) | collective-permute-done | bytes 229408 | tf_op jit(solution)/shard_map/ppermute | solution.py:309
  40.2 0.1 broadcast_select_fusion
  40.3 4.5 %collective-permute-start.11 = (bf16[128,896]{1,0:T(8,128)(2,1)S(1)}, bf16[128,896]{1,0:T(8,128)(2,1)S(1)}, u32[]{:S(2)}, u32[]{:S(2)}) collective-permute-start(bf16[128,896]{1,0:T(8,128)(2,1)S(1)} %get-tuple-element.105), channel_id=1, source_target_pairs={{0,4},{4,8},{8,12},{12,16},{16,20},{20,24},{24,28},{28,0},{1,5},{5... | collective-permute-start | bytes 688136 | tf_op jit(solution)/shard_map/ppermute | solution.py:334
  44.9 0.2 scatter.20
  45.1 0.1 bitcast_dynamic-update-slice_fusion.3
  45.2 0.0 collective-permute-done.9
  45.2 0.1 fusion
  45.3 1.6 %collective-permute-start.10 = (bf16[128,896]{1,0:T(8,128)(2,1)S(1)}, bf16[128,896]{1,0:T(8,128)(2,1)S(1)}, u32[]{:S(2)}, u32[]{:S(2)}) collective-permute-start(bf16[128,896]{1,0:T(8,128)(2,1)S(1)} %fusion), channel_id=1, source_target_pairs={{0,2},{1,3},{2,0},{3,1},{4,6},{5,7},{6,4},{7,5},{8,10},{9,11},{10,... | collective-permute-start | bytes 688136 | tf_op jit(solution)/shard_map/ppermute | solution.py:309
  46.8 3.6 %collective-permute-done.6 = bf16[128,896]{1,0:T(8,128)(2,1)S(1)} collective-permute-done((bf16[128,896]{1,0:T(8,128)(2,1)S(1)}, bf16[128,896]{1,0:T(8,128)(2,1)S(1)}, u32[]{:S(2)}, u32[]{:S(2)}) %collective-permute-start.6) | collective-permute-done | bytes 229408 | tf_op jit(solution)/shard_map/ppermute | solution.py:328
  50.5 0.0 collective-permute-done.7
  50.5 1.7 %collective-permute-done.10 = bf16[128,896]{1,0:T(8,128)(2,1)S(1)} collective-permute-done((bf16[128,896]{1,0:T(8,128)(2,1)S(1)}, bf16[128,896]{1,0:T(8,128)(2,1)S(1)}, u32[]{:S(2)}, u32[]{:S(2)}) %collective-permute-start.10) | collective-permute-done | bytes 229408 | tf_op jit(solution)/shard_map/ppermute | solution.py:309
  52.2 0.1 fusion.13
  52.3 0.0 copy-start.1
  52.3 0.0 collective-permute-done.11
  52.3 1.2 %copy-done.1 = bf16[8,128,896]{2,1,0:T(8,128)(2,1)} copy-done((bf16[8,128,896]{2,1,0:T(8,128)(2,1)}, bf16[8,128,896]{2,1,0:T(8,128)(2,1)S(1)}, u32[]{:S(2)}) %copy-start.1) | copy-done | bytes 1835032
  53.5 0.7 %bitcast_dynamic-update-slice_fusion = bf16[8,128,896]{2,1,0:T(8,128)(2,1)} fusion(bf16[8,128,896]{2,1,0:T(8,128)(2,1)} %copy-done.1, bf16[128,896]{1,0:T(8,128)(2,1)S(1)} %collective-permute-done.11), kind=kLoop, calls=%fused_computation.30 | loop fusion | bytes 458752 | tf_op jit(solution)/shard_map/scatter | solution.py:340
  (3 shorter events, 0.1 us)
Async XLA Ops:
  0.0 0.7 %copy-start = (s32[4]{0:T(128)S(1)}, s32[4]{0:T(128)}, u32[]{:S(2)}) copy-start(s32[4]{0:T(128)} %live_ref.3) | copy-start | bytes 52
  12.6 9.7 %collective-permute-start = (bf16[2,128,896]{2,1,0:T(8,128)(2,1)S(1)}, bf16[2,128,896]{2,1,0:T(8,128)(2,1)S(1)}, u32[]{:S(2)}, u32[]{:S(2)}) collective-permute-start(bf16[2,128,896]{2,1,0:T(8,128)(2,1)S(1)} %get-tuple-element.92), channel_id=1, source_target_pairs={{0,1},{1,0},{2,3},{3,2},{4,5},{5,4},{6,7},{7,6},{8,9},{9,8},{10,11... | collective-permute-start | bytes 1376264 | tf_op jit(solution)/shard_map/ppermute | solution.py:307
  13.2 10.7 %collective-permute-start.4 = (bf16[2,128,896]{2,1,0:T(8,128)(2,1)S(1)}, bf16[2,128,896]{2,1,0:T(8,128)(2,1)S(1)}, u32[]{:S(2)}, u32[]{:S(2)}) collective-permute-start(bf16[2,128,896]{2,1,0:T(8,128)(2,1)S(1)} %get-tuple-element.99), channel_id=1, source_target_pairs={{0,1},{1,0},{2,3},{3,2},{4,5},{5,4},{6,7},{7,6},{8,9},{9,8},{10,11... | collective-permute-start | bytes 1376264 | tf_op jit(solution)/shard_map/ppermute | solution.py:307
  13.2 16.0 %collective-permute-start.8 = (bf16[2,128,896]{2,1,0:T(8,128)(2,1)S(1)}, bf16[2,128,896]{2,1,0:T(8,128)(2,1)S(1)}, u32[]{:S(2)}, u32[]{:S(2)}) collective-permute-start(bf16[2,128,896]{2,1,0:T(8,128)(2,1)S(1)} %get-tuple-element.101), channel_id=1, source_target_pairs={{0,4},{4,8},{8,12},{12,16},{16,20},{20,24},{24,28},{28,0},{1,5},{5... | collective-permute-start | bytes 1376264 | tf_op jit(solution)/shard_map/ppermute | solution.py:317
  20.9 9.6 %collective-permute-start.2 = (bf16[2,128,896]{2,1,0:T(8,128)(2,1)S(1)}, bf16[2,128,896]{2,1,0:T(8,128)(2,1)S(1)}, u32[]{:S(2)}, u32[]{:S(2)}) collective-permute-start(bf16[2,128,896]{2,1,0:T(8,128)(2,1)S(1)} %get-tuple-element.96), channel_id=1, source_target_pairs={{0,1},{1,0},{2,3},{3,2},{4,5},{5,4},{6,7},{7,6},{8,9},{9,8},{10,11... | collective-permute-start | bytes 1376264 | tf_op jit(solution)/shard_map/ppermute | solution.py:307
  22.3 10.4 %collective-permute-start.1 = (bf16[128,896]{1,0:T(8,128)(2,1)S(1)}, bf16[128,896]{1,0:T(8,128)(2,1)S(1)}, u32[]{:S(2)}, u32[]{:S(2)}) collective-permute-start(bf16[128,896]{1,0:T(8,128)(2,1)S(1)} %fusion.9), channel_id=1, source_target_pairs={{0,2},{1,3},{2,0},{3,1},{4,6},{5,7},{6,4},{7,5},{8,10},{9,11},{10,... | collective-permute-start | bytes 688136 | tf_op jit(solution)/shard_map/ppermute | solution.py:309
  24.0 11.8 %collective-permute-start.5 = (bf16[128,896]{1,0:T(8,128)(2,1)S(1)}, bf16[128,896]{1,0:T(8,128)(2,1)S(1)}, u32[]{:S(2)}, u32[]{:S(2)}) collective-permute-start(bf16[128,896]{1,0:T(8,128)(2,1)S(1)} %fusion.3), channel_id=1, source_target_pairs={{0,2},{1,3},{2,0},{3,1},{4,6},{5,7},{6,4},{7,5},{8,10},{9,11},{10,... | collective-permute-start | bytes 688136 | tf_op jit(solution)/shard_map/ppermute | solution.py:309
  30.4 14.8 %collective-permute-start.9 = (bf16[2,128,896]{2,1,0:T(8,128)(2,1)S(1)}, bf16[2,128,896]{2,1,0:T(8,128)(2,1)S(1)}, u32[]{:S(2)}, u32[]{:S(2)}) collective-permute-start(bf16[2,128,896]{2,1,0:T(8,128)(2,1)S(1)} %get-tuple-element.103), channel_id=1, source_target_pairs={{0,1},{1,0},{2,3},{3,2},{4,5},{5,4},{6,7},{7,6},{8,9},{9,8},{10,11... | collective-permute-start | bytes 1376264 | tf_op jit(solution)/shard_map/ppermute | solution.py:307
  30.5 9.7 %collective-permute-start.3 = (bf16[128,896]{1,0:T(8,128)(2,1)S(1)}, bf16[128,896]{1,0:T(8,128)(2,1)S(1)}, u32[]{:S(2)}, u32[]{:S(2)}) collective-permute-start(bf16[128,896]{1,0:T(8,128)(2,1)S(1)} %fusion.6), channel_id=1, source_target_pairs={{0,2},{1,3},{2,0},{3,1},{4,6},{5,7},{6,4},{7,5},{8,10},{9,11},{10,... | collective-permute-start | bytes 688136 | tf_op jit(solution)/shard_map/ppermute | solution.py:309
  32.8 17.6 %collective-permute-start.7 = (bf16[128,896]{1,0:T(8,128)(2,1)S(1)}, bf16[128,896]{1,0:T(8,128)(2,1)S(1)}, u32[]{:S(2)}, u32[]{:S(2)}) collective-permute-start(bf16[128,896]{1,0:T(8,128)(2,1)S(1)} %get-tuple-element.107), channel_id=1, source_target_pairs={{0,28},{4,0},{8,4},{12,8},{16,12},{20,16},{24,20},{28,24},{1,29},{... | collective-permute-start | bytes 688136 | tf_op jit(solution)/shard_map/ppermute | solution.py:331
  35.9 14.6 %collective-permute-start.6 = (bf16[128,896]{1,0:T(8,128)(2,1)S(1)}, bf16[128,896]{1,0:T(8,128)(2,1)S(1)}, u32[]{:S(2)}, u32[]{:S(2)}) collective-permute-start(bf16[128,896]{1,0:T(8,128)(2,1)S(1)} %fusion.5), channel_id=1, source_target_pairs={{0,28},{4,0},{8,4},{12,8},{16,12},{20,16},{24,20},{28,24},{1,29},{... | collective-permute-start | bytes 688136 | tf_op jit(solution)/shard_map/ppermute | solution.py:328
  40.3 12.0 %collective-permute-start.11 = (bf16[128,896]{1,0:T(8,128)(2,1)S(1)}, bf16[128,896]{1,0:T(8,128)(2,1)S(1)}, u32[]{:S(2)}, u32[]{:S(2)}) collective-permute-start(bf16[128,896]{1,0:T(8,128)(2,1)S(1)} %get-tuple-element.105), channel_id=1, source_target_pairs={{0,4},{4,8},{8,12},{12,16},{16,20},{20,24},{24,28},{28,0},{1,5},{5... | collective-permute-start | bytes 688136 | tf_op jit(solution)/shard_map/ppermute | solution.py:334
  45.3 6.9 %collective-permute-start.10 = (bf16[128,896]{1,0:T(8,128)(2,1)S(1)}, bf16[128,896]{1,0:T(8,128)(2,1)S(1)}, u32[]{:S(2)}, u32[]{:S(2)}) collective-permute-start(bf16[128,896]{1,0:T(8,128)(2,1)S(1)} %fusion), channel_id=1, source_target_pairs={{0,2},{1,3},{2,0},{3,1},{4,6},{5,7},{6,4},{7,5},{8,10},{9,11},{10,... | collective-permute-start | bytes 688136 | tf_op jit(solution)/shard_map/ppermute | solution.py:309
  52.3 1.2 %copy-start.1 = (bf16[8,128,896]{2,1,0:T(8,128)(2,1)}, bf16[8,128,896]{2,1,0:T(8,128)(2,1)S(1)}, u32[]{:S(2)}) copy-start(bf16[8,128,896]{2,1,0:T(8,128)(2,1)S(1)} %fusion.13) | copy-start | bytes 5505028

commit v5 on v4

--- a/solution.py
+++ b/solution.py
@@ -292,8 +292,10 @@
     left, right = left_count[0], right_count[0]
     zero = jnp.zeros((), jnp.bfloat16)
 
-    in_hbm = [kv_keys, kv_values, queries, hidden, out_weight, node_tiles]
-    kv_keys, kv_values, queries, hidden, out_weight, node_tiles = [
+    in_hbm = [kv_keys, kv_values, queries, hidden, out_weight, node_tiles, block_live]
+    (
+        kv_keys, kv_values, queries, hidden, out_weight, node_tiles, block_live
+    ) = [
         pltpu.with_memory_space_constraint(a, pltpu.HBM) for a in in_hbm
     ]
 

time: 54.5 us -> 54.1 us (level)
  local copies, waits for them, and re-layouts: 2.85 us -> 2.19 us
    ppermute x4, waiting for transfers between devices: 4.22 us -> 7.84 us  [sum_start(): return (got[0], lax.ppermute(across, 'tp', to_across))]
    ppermute x1, waiting for transfers between devices: 3.61 us -> 0.01 us  [on_device(): lax.ppermute(total(mine0, mates0, other0).astype(bf16), 'blk', to_prev)]
    unnamed x4 -> x2, local copies, waits for them, and re-layouts: 1.87 us -> 1.21 us
  transfers between devices with their start and end apart: 12 -> 12, of which waited for: 5 -> 4; matrix products, arithmetic and copies ran while one was open for 2% -> 2% of each run, Pallas kernels for 12% -> 12%
where the time goes in v5:
time: 54.1 us; the launch traced here: 53.8 us
  Pallas kernels  18.6 us (34%)
  starting transfers between devices  18.6 us (34%)
  waiting for transfers between devices  12.4 us (23%)
  local copies, waits for them, and re-layouts  2.19 us (4%)
  between operations  1.47 us (3%)
  other arithmetic  0.65 us (1%)
    pallas_call x2, Pallas kernels, attend_blocks(): pl.pallas_call(functools.partial(attend_kernel, ids, shipped), grid_spec=...  17.5 us
    ppermute x4, waiting for transfers between devices, sum_start(): return (got[0], lax.ppermute(across, 'tp', to_across))  7.84 us
    ppermute x4, starting transfers between devices, sum_start(): return (got[0], lax.ppermute(across, 'tp', to_across))  5.93 us
    ppermute x1, starting transfers between devices, on_device(): lax.ppermute(masked(result, blocks - 2 <= right), 'blk', to_next)  4.53 us
    ppermute x1, waiting for transfers between devices, on_device(): moved = lax.ppermute(ship, 'blk', to_next)  4.49 us
    ppermute x1, starting transfers between devices, on_device(): lax.ppermute(total(mine0, mates0, other0).astype(bf16), 'blk', to_prev)  3.33 us
    ppermute x1, starting transfers between devices, on_device(): moved = lax.ppermute(ship, 'blk', to_next)  2.35 us
    ppermute x1, starting transfers between devices, on_device(): from_next1 = lax.ppermute(masked(result, 1 < left), 'blk', to_prev)  1.64 us
  transfers between devices with their start and end apart: 12, of which 4 were waited for; matrix products, arithmetic and copies ran while one was open for 2% of the time, Pallas kernels for 12%

profile of v5, /device:TPU:0, one launch (start us, length us, event | category | flops | bytes accessed | tf_op | source)
XLA Modules:
  0.0 53.8 jit_solution(5561759954782516010)
XLA Ops:
  0.0 12.0 %shard_map.91 = (bf16[2,128,896]{2,1,0:T(8,128)(2,1)S(1)}, bf16[2,128,896]{2,1,0:T(8,128)(2,1)S(1)}, bf16[128,896]{1,0:T(8,128)(2,1)S(1)}, bf16[128,896]{1,0:T(8...) custom-call(s32[4]{0:T(128)} %live_ref.3, ...), custom_call_target="tpu_custom_call" | custom-call | flops 4462739456 | bytes 9568256 | tf_op jit(solution)/shard_map/pallas_call | solution.py:251
  12.0 0.6 %collective-permute-start = (bf16[2,128,896]{2,1,0:T(8,128)(2,1)S(1)}, bf16[2,128,896]{2,1,0:T(8,128)(2,1)S(1)}, u32[]{:S(2)}, u32[]{:S(2)}) collective-permute-start(bf16[2,128,896]{2,1,0:T(8,128)(2,1)S(1)} %get-tuple-element.92), channel_id=1, source_target_pairs={{0,1},{1,0},{2,3},{3,2},{4,5},{5,4},{6,7},{7,6},{8,9},{9,8},{10,11... | collective-permute-start | bytes 1376264 | tf_op jit(solution)/shard_map/ppermute | solution.py:309
  12.6 0.1 collective-permute-start.4
  12.7 2.3 %collective-permute-start.8 = (bf16[2,128,896]{2,1,0:T(8,128)(2,1)S(1)}, bf16[2,128,896]{2,1,0:T(8,128)(2,1)S(1)}, u32[]{:S(2)}, u32[]{:S(2)}) collective-permute-start(bf16[2,128,896]{2,1,0:T(8,128)(2,1)S(1)} %get-tuple-element.101), channel_id=1, source_target_pairs={{0,4},{4,8},{8,12},{12,16},{16,20},{20,24},{24,28},{28,0},{1,5},{5... | collective-permute-start | bytes 1376264 | tf_op jit(solution)/shard_map/ppermute | solution.py:319
  15.0 5.4 %shard_map.92 = (bf16[2,128,896]{2,1,0:T(8,128)(2,1)S(1)}, bf16[128,896]{1,0:T(8,128)(2,1)S(1)}, f32[128,896]{1,0:T(8,128)S(1)}) custom-call(s32[4]{0:T(128)} %live_ref.3, bf16[4,128,896]{2,1,0:T(8,128)(2,1)} %q_hbm.3, bf16[4,2048,128]{2,1,0:T(8,128)(2,1)} %k_hbm.3, bf16[4,2048,128]{2,1,0:T(8,128)(2,1)} %v_hbm.3, bf16[4,128,896]{2,1,0:T(8,128)(2,1)} %hidden_hbm.3, ...), custom_call_target="tpu_custom_call" | custom-call | flops 1761607680 | bytes 7471104 | tf_op jit(solution)/shard_map/pallas_call | solution.py:251
  20.5 0.1 collective-permute-start.2
  21.9 0.0 collective-permute-done
  21.9 0.1 fusion.9
  21.9 1.6 %collective-permute-start.1 = (bf16[128,896]{1,0:T(8,128)(2,1)S(1)}, bf16[128,896]{1,0:T(8,128)(2,1)S(1)}, u32[]{:S(2)}, u32[]{:S(2)}) collective-permute-start(bf16[128,896]{1,0:T(8,128)(2,1)S(1)} %fusion.9), channel_id=1, source_target_pairs={{0,2},{1,3},{2,0},{3,1},{4,6},{5,7},{6,4},{7,5},{8,10},{9,11},{10,... | collective-permute-start | bytes 688136 | tf_op jit(solution)/shard_map/ppermute | solution.py:311
  23.5 0.0 collective-permute-done.4
  23.5 0.1 fusion.3
  23.6 0.6 %collective-permute-start.5 = (bf16[128,896]{1,0:T(8,128)(2,1)S(1)}, bf16[128,896]{1,0:T(8,128)(2,1)S(1)}, u32[]{:S(2)}, u32[]{:S(2)}) collective-permute-start(bf16[128,896]{1,0:T(8,128)(2,1)S(1)} %fusion.3), channel_id=1, source_target_pairs={{0,2},{1,3},{2,0},{3,1},{4,6},{5,7},{6,4},{7,5},{8,10},{9,11},{10,... | collective-permute-start | bytes 688136 | tf_op jit(solution)/shard_map/ppermute | solution.py:311
  24.2 4.5 %collective-permute-done.8.moved_ref = bf16[2,128,896]{2,1,0:T(8,128)(2,1)S(1)} collective-permute-done((bf16[2,128,896]{2,1,0:T(8,128)(2,1)S(1)}, bf16[2,128,896]{2,1,0:T(8,128)(2,1)S(1)}, u32[]{:S(2)}, u32[]{:S(2)}) %collective-permute-start.8) | collective-permute-done | bytes 458784 | tf_op jit(solution)/shard_map/ppermute | solution.py:319
  28.6 1.1 %shard_map.93 = (bf16[2,128,896]{2,1,0:T(8,128)(2,1)S(1)}, bf16[128,896]{1,0:T(8,128)(2,1)S(1)}, f32[128,896]{1,0:T(8,128)S(1)}) custom-call(bf16[2,128,896]{2,1,0:T(8,128)(2,1)S(1)} %collective-permute-done.8.moved_ref, bf16[2,896,1792]{2,1,0:T(8,128)(2,1)S(1)} %get-tuple-element.94.w_hbm.w_ref), custom_call_target="tpu_custom_call" | custom-call | flops 1644167168 | bytes 6422528 | tf_op jit(solution)/shard_map/pallas_call | solution.py:268
  29.8 0.1 collective-permute-start.9
  29.9 0.0 collective-permute-done.2
  29.9 0.1 fusion.6
  29.9 2.2 %collective-permute-start.3 = (bf16[128,896]{1,0:T(8,128)(2,1)S(1)}, bf16[128,896]{1,0:T(8,128)(2,1)S(1)}, u32[]{:S(2)}, u32[]{:S(2)}) collective-permute-start(bf16[128,896]{1,0:T(8,128)(2,1)S(1)} %fusion.6), channel_id=1, source_target_pairs={{0,2},{1,3},{2,0},{3,1},{4,6},{5,7},{6,4},{7,5},{8,10},{9,11},{10,... | collective-permute-start | bytes 688136 | tf_op jit(solution)/shard_map/ppermute | solution.py:311
  32.2 0.0 collective-permute-done.1
  32.2 0.1 broadcast_select_fusion.1
  32.3 1.6 %collective-permute-start.7 = (bf16[128,896]{1,0:T(8,128)(2,1)S(1)}, bf16[128,896]{1,0:T(8,128)(2,1)S(1)}, u32[]{:S(2)}, u32[]{:S(2)}) collective-permute-start(bf16[128,896]{1,0:T(8,128)(2,1)S(1)} %get-tuple-element.107), channel_id=1, source_target_pairs={{0,28},{4,0},{8,4},{12,8},{16,12},{20,16},{24,20},{28,24},{1,29},{... | collective-permute-start | bytes 688136 | tf_op jit(solution)/shard_map/ppermute | solution.py:333
  33.9 1.5 %collective-permute-done.5 = bf16[128,896]{1,0:T(8,128)(2,1)S(1)} collective-permute-done((bf16[128,896]{1,0:T(8,128)(2,1)S(1)}, bf16[128,896]{1,0:T(8,128)(2,1)S(1)}, u32[]{:S(2)}, u32[]{:S(2)}) %collective-permute-start.5) | collective-permute-done | bytes 229408 | tf_op jit(solution)/shard_map/ppermute | solution.py:311
  35.4 0.1 fusion.5
  35.5 3.3 %collective-permute-start.6 = (bf16[128,896]{1,0:T(8,128)(2,1)S(1)}, bf16[128,896]{1,0:T(8,128)(2,1)S(1)}, u32[]{:S(2)}, u32[]{:S(2)}) collective-permute-start(bf16[128,896]{1,0:T(8,128)(2,1)S(1)} %fusion.5), channel_id=1, source_target_pairs={{0,28},{4,0},{8,4},{12,8},{16,12},{20,16},{24,20},{28,24},{1,29},{... | collective-permute-start | bytes 688136 | tf_op jit(solution)/shard_map/ppermute | solution.py:330
  38.8 1.0 %collective-permute-done.3 = bf16[128,896]{1,0:T(8,128)(2,1)S(1)} collective-permute-done((bf16[128,896]{1,0:T(8,128)(2,1)S(1)}, bf16[128,896]{1,0:T(8,128)(2,1)S(1)}, u32[]{:S(2)}, u32[]{:S(2)}) %collective-permute-start.3) | collective-permute-done | bytes 229408 | tf_op jit(solution)/shard_map/ppermute | solution.py:311
  39.8 0.1 broadcast_select_fusion
  39.9 4.5 %collective-permute-start.11 = (bf16[128,896]{1,0:T(8,128)(2,1)S(1)}, bf16[128,896]{1,0:T(8,128)(2,1)S(1)}, u32[]{:S(2)}, u32[]{:S(2)}) collective-permute-start(bf16[128,896]{1,0:T(8,128)(2,1)S(1)} %get-tuple-element.105), channel_id=1, source_target_pairs={{0,4},{4,8},{8,12},{12,16},{16,20},{20,24},{24,28},{28,0},{1,5},{5... | collective-permute-start | bytes 688136 | tf_op jit(solution)/shard_map/ppermute | solution.py:336
  44.5 0.2 scatter.20
  44.7 0.1 bitcast_dynamic-update-slice_fusion.3
  44.8 0.0 collective-permute-done.9
  44.8 0.1 fusion
  44.9 1.6 %collective-permute-start.10 = (bf16[128,896]{1,0:T(8,128)(2,1)S(1)}, bf16[128,896]{1,0:T(8,128)(2,1)S(1)}, u32[]{:S(2)}, u32[]{:S(2)}) collective-permute-start(bf16[128,896]{1,0:T(8,128)(2,1)S(1)} %fusion), channel_id=1, source_target_pairs={{0,2},{1,3},{2,0},{3,1},{4,6},{5,7},{6,4},{7,5},{8,10},{9,11},{10,... | collective-permute-start | bytes 688136 | tf_op jit(solution)/shard_map/ppermute | solution.py:311
  46.4 0.0 collective-permute-done.6
  46.5 0.0 collective-permute-done.7
  46.5 5.3 %collective-permute-done.10 = bf16[128,896]{1,0:T(8,128)(2,1)S(1)} collective-permute-done((bf16[128,896]{1,0:T(8,128)(2,1)S(1)}, bf16[128,896]{1,0:T(8,128)(2,1)S(1)}, u32[]{:S(2)}, u32[]{:S(2)}) %collective-permute-start.10) | collective-permute-done | bytes 229408 | tf_op jit(solution)/shard_map/ppermute | solution.py:311
  51.8 0.1 fusion.13
  51.9 0.0 copy-start
  51.9 0.0 collective-permute-done.11
  51.9 1.2 %copy-done = bf16[8,128,896]{2,1,0:T(8,128)(2,1)} copy-done((bf16[8,128,896]{2,1,0:T(8,128)(2,1)}, bf16[8,128,896]{2,1,0:T(8,128)(2,1)S(1)}, u32[]{:S(2)}) %copy-start) | copy-done | bytes 1835032
  53.1 0.7 %bitcast_dynamic-update-slice_fusion = bf16[8,128,896]{2,1,0:T(8,128)(2,1)} fusion(bf16[8,128,896]{2,1,0:T(8,128)(2,1)} %copy-done, bf16[128,896]{1,0:T(8,128)(2,1)S(1)} %collective-permute-done.11), kind=kLoop, calls=%fused_computation.30 | loop fusion | bytes 458752 | tf_op jit(solution)/shard_map/scatter | solution.py:342
  (3 shorter events, 0.1 us)
Async XLA Ops:
  12.0 9.8 %collective-permute-start = (bf16[2,128,896]{2,1,0:T(8,128)(2,1)S(1)}, bf16[2,128,896]{2,1,0:T(8,128)(2,1)S(1)}, u32[]{:S(2)}, u32[]{:S(2)}) collective-permute-start(bf16[2,128,896]{2,1,0:T(8,128)(2,1)S(1)} %get-tuple-element.92), channel_id=1, source_target_pairs={{0,1},{1,0},{2,3},{3,2},{4,5},{5,4},{6,7},{7,6},{8,9},{9,8},{10,11... | collective-permute-start | bytes 1376264 | tf_op jit(solution)/shard_map/ppermute | solution.py:309
  12.6 10.9 %collective-permute-start.4 = (bf16[2,128,896]{2,1,0:T(8,128)(2,1)S(1)}, bf16[2,128,896]{2,1,0:T(8,128)(2,1)S(1)}, u32[]{:S(2)}, u32[]{:S(2)}) collective-permute-start(bf16[2,128,896]{2,1,0:T(8,128)(2,1)S(1)} %get-tuple-element.99), channel_id=1, source_target_pairs={{0,1},{1,0},{2,3},{3,2},{4,5},{5,4},{6,7},{7,6},{8,9},{9,8},{10,11... | collective-permute-start | bytes 1376264 | tf_op jit(solution)/shard_map/ppermute | solution.py:309
  12.7 16.0 %collective-permute-start.8 = (bf16[2,128,896]{2,1,0:T(8,128)(2,1)S(1)}, bf16[2,128,896]{2,1,0:T(8,128)(2,1)S(1)}, u32[]{:S(2)}, u32[]{:S(2)}) collective-permute-start(bf16[2,128,896]{2,1,0:T(8,128)(2,1)S(1)} %get-tuple-element.101), channel_id=1, source_target_pairs={{0,4},{4,8},{8,12},{12,16},{16,20},{20,24},{24,28},{28,0},{1,5},{5... | collective-permute-start | bytes 1376264 | tf_op jit(solution)/shard_map/ppermute | solution.py:319
  20.5 9.4 %collective-permute-start.2 = (bf16[2,128,896]{2,1,0:T(8,128)(2,1)S(1)}, bf16[2,128,896]{2,1,0:T(8,128)(2,1)S(1)}, u32[]{:S(2)}, u32[]{:S(2)}) collective-permute-start(bf16[2,128,896]{2,1,0:T(8,128)(2,1)S(1)} %get-tuple-element.96), channel_id=1, source_target_pairs={{0,1},{1,0},{2,3},{3,2},{4,5},{5,4},{6,7},{7,6},{8,9},{9,8},{10,11... | collective-permute-start | bytes 1376264 | tf_op jit(solution)/shard_map/ppermute | solution.py:309
  21.9 10.2 %collective-permute-start.1 = (bf16[128,896]{1,0:T(8,128)(2,1)S(1)}, bf16[128,896]{1,0:T(8,128)(2,1)S(1)}, u32[]{:S(2)}, u32[]{:S(2)}) collective-permute-start(bf16[128,896]{1,0:T(8,128)(2,1)S(1)} %fusion.9), channel_id=1, source_target_pairs={{0,2},{1,3},{2,0},{3,1},{4,6},{5,7},{6,4},{7,5},{8,10},{9,11},{10,... | collective-permute-start | bytes 688136 | tf_op jit(solution)/shard_map/ppermute | solution.py:311
  23.6 11.8 %collective-permute-start.5 = (bf16[128,896]{1,0:T(8,128)(2,1)S(1)}, bf16[128,896]{1,0:T(8,128)(2,1)S(1)}, u32[]{:S(2)}, u32[]{:S(2)}) collective-permute-start(bf16[128,896]{1,0:T(8,128)(2,1)S(1)} %fusion.3), channel_id=1, source_target_pairs={{0,2},{1,3},{2,0},{3,1},{4,6},{5,7},{6,4},{7,5},{8,10},{9,11},{10,... | collective-permute-start | bytes 688136 | tf_op jit(solution)/shard_map/ppermute | solution.py:311
  29.8 15.0 %collective-permute-start.9 = (bf16[2,128,896]{2,1,0:T(8,128)(2,1)S(1)}, bf16[2,128,896]{2,1,0:T(8,128)(2,1)S(1)}, u32[]{:S(2)}, u32[]{:S(2)}) collective-permute-start(bf16[2,128,896]{2,1,0:T(8,128)(2,1)S(1)} %get-tuple-element.103), channel_id=1, source_target_pairs={{0,1},{1,0},{2,3},{3,2},{4,5},{5,4},{6,7},{7,6},{8,9},{9,8},{10,11... | collective-permute-start | bytes 1376264 | tf_op jit(solution)/shard_map/ppermute | solution.py:309
  29.9 9.9 %collective-permute-start.3 = (bf16[128,896]{1,0:T(8,128)(2,1)S(1)}, bf16[128,896]{1,0:T(8,128)(2,1)S(1)}, u32[]{:S(2)}, u32[]{:S(2)}) collective-permute-start(bf16[128,896]{1,0:T(8,128)(2,1)S(1)} %fusion.6), channel_id=1, source_target_pairs={{0,2},{1,3},{2,0},{3,1},{4,6},{5,7},{6,4},{7,5},{8,10},{9,11},{10,... | collective-permute-start | bytes 688136 | tf_op jit(solution)/shard_map/ppermute | solution.py:311
  32.3 14.2 %collective-permute-start.7 = (bf16[128,896]{1,0:T(8,128)(2,1)S(1)}, bf16[128,896]{1,0:T(8,128)(2,1)S(1)}, u32[]{:S(2)}, u32[]{:S(2)}) collective-permute-start(bf16[128,896]{1,0:T(8,128)(2,1)S(1)} %get-tuple-element.107), channel_id=1, source_target_pairs={{0,28},{4,0},{8,4},{12,8},{16,12},{20,16},{24,20},{28,24},{1,29},{... | collective-permute-start | bytes 688136 | tf_op jit(solution)/shard_map/ppermute | solution.py:333
  35.5 11.0 %collective-permute-start.6 = (bf16[128,896]{1,0:T(8,128)(2,1)S(1)}, bf16[128,896]{1,0:T(8,128)(2,1)S(1)}, u32[]{:S(2)}, u32[]{:S(2)}) collective-permute-start(bf16[128,896]{1,0:T(8,128)(2,1)S(1)} %fusion.5), channel_id=1, source_target_pairs={{0,28},{4,0},{8,4},{12,8},{16,12},{20,16},{24,20},{28,24},{1,29},{... | collective-permute-start | bytes 688136 | tf_op jit(solution)/shard_map/ppermute | solution.py:330
  39.9 12.0 %collective-permute-start.11 = (bf16[128,896]{1,0:T(8,128)(2,1)S(1)}, bf16[128,896]{1,0:T(8,128)(2,1)S(1)}, u32[]{:S(2)}, u32[]{:S(2)}) collective-permute-start(bf16[128,896]{1,0:T(8,128)(2,1)S(1)} %get-tuple-element.105), channel_id=1, source_target_pairs={{0,4},{4,8},{8,12},{12,16},{16,20},{20,24},{24,28},{28,0},{1,5},{5... | collective-permute-start | bytes 688136 | tf_op jit(solution)/shard_map/ppermute | solution.py:336
  44.9 6.9 %collective-permute-start.10 = (bf16[128,896]{1,0:T(8,128)(2,1)S(1)}, bf16[128,896]{1,0:T(8,128)(2,1)S(1)}, u32[]{:S(2)}, u32[]{:S(2)}) collective-permute-start(bf16[128,896]{1,0:T(8,128)(2,1)S(1)} %fusion), channel_id=1, source_target_pairs={{0,2},{1,3},{2,0},{3,1},{4,6},{5,7},{6,4},{7,5},{8,10},{9,11},{10,... | collective-permute-start | bytes 688136 | tf_op jit(solution)/shard_map/ppermute | solution.py:311
  51.9 1.2 %copy-start = (bf16[8,128,896]{2,1,0:T(8,128)(2,1)}, bf16[8,128,896]{2,1,0:T(8,128)(2,1)S(1)}, u32[]{:S(2)}) copy-start(bf16[8,128,896]{2,1,0:T(8,128)(2,1)S(1)} %fusion.13) | copy-start | bytes 5505028
